TPU v7x, 512 devices: a whole 4x4x16 slice. The times are simulated.
512 devices in a mesh: pair: 64 (over x, y, z_hi), sector: 8 (over z_lo, core).
Axes of the slice: x: 4, y: 4, z: 16 (z_hi: 4, z_lo: 4; z = z_hi * 4 + z_lo), core: 2. Of those that a mesh axis runs over, the one named last changes fastest.
Arguments:
- site_tensor: bfloat16 [4, 16, 128, 128], P(None, 'sector', 'pair'), may hold values from -0.5 to 0.5
- operators: bfloat16 [1536, 16, 128, 128], P('pair', 'sector'), may hold values from -6 to 6
- one_index: bfloat16 [128, 16, 128, 128], P('pair', 'sector'), may hold values from -6 to 6
- weights: bfloat16 [1536, 128], P('pair'), may hold values from -1 to 1
- comp_charge: int32 [1536], P('pair'), may hold values from 0 to 2
- one_charge: int32 [128], replicated, may hold values from 0 to 2
- sector_size: int32 [16], replicated, may hold values from 1 to 128, 1280 in all
- coupling: int32 [16, 4], replicated, may hold values from 0 to 16, as said below
Outputs:
- renormalized: bfloat16 [1536, 16, 128, 128], P('pair', 'sector')
Inputs may be any that keep to these rules, and one draw needn't show every extreme that they name: coupling[s, t] = min(s + c[t], 16) where c is an arrangement of the charges 0, 1, 1, 2 over the 4 orbital states; the value 16 marks a dropped combination.
All inputs are finite; a program needn't handle non-finite values.
Results may differ from a plain program's by a relative error of at most 0.007.
Values may be sent and summed in bfloat16 or wider, within the bound.
No kernel may reach another device: no remote copies, remote signals or barrier semaphores. Data moves between devices by JAX's collectives and lax.ppermute only.
A program may use at most 64 MiB of HBM per device.

v0:
```python
import jax
import jax.numpy as jnp
from jax import lax
from jax.experimental import pallas as pl
from jax.experimental.pallas import tpu as pltpu
from jax.sharding import Mesh, PartitionSpec as P

F32 = jnp.float32
BF16 = jnp.bfloat16
PLANE = ("x", "y")
GROUP = ("zl", "core")
VMEM = pl.BlockSpec(memory_space=pltpu.VMEM)
SMEM = pl.BlockSpec(memory_space=pltpu.SMEM)
HBM = pl.BlockSpec(memory_space=pltpu.MemorySpace.HBM)
DMA = pltpu.SemaphoreType.DMA
COEF_AT, SITE_AT, MESSAGE = 128, 160, 224


def call(body, out, ins, outs, scratch=(), flops=0, moved=4 << 20, grant=16 << 20, **more):
    return pl.pallas_call(
        body,
        out_shape=out,
        in_specs=ins,
        out_specs=outs,
        scratch_shapes=list(scratch),
        cost_estimate=pl.CostEstimate(flops=flops, bytes_accessed=moved, transcendentals=0),
        compiler_params=pltpu.CompilerParams(vmem_limit_bytes=grant),
        **more,
    )


def shift(value, steps):
    count = lax.axis_size(GROUP)
    first, last = max(0, -steps), min(count, count - steps)
    return lax.ppermute(value, GROUP, [(a, a + steps) for a in range(first, last)])


def spread_kernel(c_ref, g_ref, out_ref, sf_ref):
    planes = out_ref.shape[0]
    for half in range(2):
        for zh in range(4):
            parts = []
            for j in range(2):
                at = (j * 2 + 1 - half) * 128
                parts.append(g_ref[zh, at : at + 128, :].astype(F32).reshape(planes, 8, 128))
            to = half * 64 + zh * 16
            out_ref[:, to : to + 16, :] = jnp.concatenate(parts, axis=1).astype(BF16)
    for zh in range(4):
        piece = g_ref[zh, 512:528, :].astype(F32)
        for b in range(8):
            sf_ref[b * 8 + zh * 2 : b * 8 + zh * 2 + 2, :] = piece[2 * b : 2 * b + 2, :]
    site = sf_ref[...].astype(BF16)
    coef = c_ref[...].astype(F32)
    coef = jnp.concatenate([coef, jnp.zeros((SITE_AT - COEF_AT - c_ref.shape[0], 128), F32)], axis=0).astype(BF16)
    for d in range(planes):
        out_ref[d, COEF_AT:SITE_AT, :] = coef
        out_ref[d, SITE_AT:, :] = site


def mix(half, a_ref, out_ref, gf_ref, cf_ref):
    planes, rows = out_ref.shape[:2]
    ops = rows // 8
    coef = a_ref[:, COEF_AT : COEF_AT + ops, :].astype(F32).reshape(planes * ops, 128).astype(BF16)
    gf_ref[...] = a_ref[:, half * 64 : half * 64 + 64, :].astype(F32).reshape(1024, 128)
    for r in range(8):
        block = gf_ref[pl.ds(r, 128, stride=8), :].astype(BF16)
        cf_ref[pl.ds(r, planes * ops, stride=8), :] = jnp.dot(coef, block, preferred_element_type=F32)

    def finish(d, _):
        at = pl.multiple_of(d * rows, 16)
        out_ref[d] = cf_ref[pl.ds(at, rows), :].astype(BF16)
        return 0

    lax.fori_loop(0, planes, finish, 0, unroll=4)


def mix_one(*refs):
    mix(0, *refs)


def mix_zero(*refs):
    mix(1, *refs)


def state_order(coupling_ref):
    c = [coupling_ref[0, t] for t in range(4)]
    zero, two, low, high = (jnp.int32(0) for _ in range(4))
    for t in range(4):
        zero = jnp.where(c[t] == 0, t, zero)
        two = jnp.where(c[t] == 2, t, two)
        high = jnp.where(c[t] == 1, t, high)
    for t in reversed(range(4)):
        low = jnp.where(c[t] == 1, t, low)
    return [zero, low, high, two]


def site_kernel(coupling_ref, size_ref, a_ref, own_ref):
    first = 4 * lax.axis_index("zl") + 2 * lax.axis_index("core")
    line = lax.broadcasted_iota(jnp.int32, (128, 128), 0)
    order = state_order(coupling_ref)
    for n in range(4):
        at = pl.multiple_of(SITE_AT + order[n] * 16, 16)
        both = a_ref[:, pl.ds(at, 16), :].astype(F32)
        for s in range(2):
            block = both[:, s * 8 : (s + 1) * 8, :].reshape(128, 128)
            block = jnp.where(line < size_ref[first + s], block, 0.0)
            own_ref[s, :, n * 128 : (n + 1) * 128] = block.astype(BF16)


def combine(r_ref, own, h):
    both = r_ref[:, pl.ds(pl.multiple_of(h * 16, 16), 16), :].astype(F32)
    pair = []
    for e in range(2):
        summed = both[:, e * 8 : (e + 1) * 8, :].reshape(128, 128)
        pair.append((own[e].astype(F32) + summed).astype(BF16))
    return pair


def inner(block, right):
    return jnp.dot(block, right, preferred_element_type=F32).astype(BF16)


def joined(parts, first, last):
    return jnp.concatenate([v[:, first:last] for v in parts], axis=1)


def stacked(parts, first):
    tall = [jnp.concatenate([v[:, first : first + 128], v[:, first + 128 : first + 256]], axis=0) for v in parts]
    return jnp.concatenate(tall, axis=1)


def product(left, right):
    return jnp.dot(left, right, preferred_element_type=F32)


def turned(pool_ref, s, states):
    blocks = [pool_ref[s, :, n * 128 : (n + 1) * 128].astype(F32).T for n in states]
    return jnp.concatenate(blocks, axis=1).astype(BF16)


def pool_kernel(own_ref, up_ref, pool_ref, early_ref, last_ref):
    for s in range(2):
        pool_ref[s] = own_ref[s]
        pool_ref[2 + s] = up_ref[s]
        early_ref[1 + s] = up_ref[s, :, 384:]
        last_ref[s] = own_ref[s, :, 384:]
    early_ref[0] = own_ref[1, :, 384:]
    early_ref[3] = turned(own_ref, 1, (3,))
    last_ref[2] = up_ref[0, :, 384:]
    last_ref[3] = turned(own_ref, 0, (3,))


def front_kernel(charge_ref, r_ref, op_ref, early_ref, out_ref, comb_ref):
    def step(h, _):
        pair = combine(r_ref, [op_ref[2 * h + e] for e in range(2)], h)
        parts = []
        for e in range(2):
            comb_ref[2 * h + e] = pair[e]
            parts.append(inner(pair[e], early_ref[charge_ref[2 * h + e]]))
        two = product(early_ref[3], joined(parts, 0, 128))
        for e in range(2):
            out_ref[2 * h + e] = two[:, e * 128 : (e + 1) * 128].astype(BF16)
        return 0

    lax.fori_loop(0, op_ref.shape[0] // 2, step, 0, unroll=12)


def middle_kernel(charge_ref, comb_ref, pool_ref, next_ref, again_ref, left_ref):
    again_ref[...] = pool_ref[...]
    left_ref[...] = turned(pool_ref, 1, (1, 2))

    def step(h, _):
        parts = [inner(comb_ref[2 * h + e], pool_ref[charge_ref[2 * h + e] + 1, :, 128:384]) for e in range(2)]
        one = product(left_ref[...], stacked(parts, 0))
        for e in range(2):
            next_ref[2 * h + e] = one[:, e * 128 : (e + 1) * 128]
        return 0

    lax.fori_loop(0, comb_ref.shape[0] // 2, step, 0, unroll=6)


def last_kernel(charge_ref, r_ref, op_ref, next_ref, last_ref, out_ref, comb_ref):
    def step(h, _):
        pair = combine(r_ref, [op_ref[2 * h + e] for e in range(2)], h)
        parts = []
        for e in range(2):
            comb_ref[2 * h + e] = pair[e]
            parts.append(inner(pair[e], last_ref[charge_ref[2 * h + e]]))
        two = product(last_ref[3], joined(parts, 0, 128))
        for e in range(2):
            k = 2 * h + e
            out_ref[k] = (two[:, e * 128 : (e + 1) * 128] + next_ref[k]).astype(BF16)
        return 0

    lax.fori_loop(0, op_ref.shape[0] // 2, step, 0, unroll=12)


def own_kernel(charge_ref, one_ref, zero_ref, pool_ref, first_ref, second_ref, left_ref):
    left_ref[...] = jnp.concatenate([turned(pool_ref, 0, (0, 1, 2)), turned(pool_ref, 1, (0,))], axis=1)

    def step(h, _):
        low, high = [], []
        for e in range(2):
            k = 2 * h + e
            q = charge_ref[k]
            low.append(inner(zero_ref[k], pool_ref[q, :, :384]))
            high.append(inner(one_ref[k], pool_ref[q + 1, :, :128]))
        first = product(left_ref[:, :128], joined(low, 0, 128))
        second = product(left_ref[:, 128:384], stacked(low, 128)) + product(left_ref[:, 384:], joined(high, 0, 128))
        for e in range(2):
            k, at = 2 * h + e, slice(e * 128, (e + 1) * 128)
            first_ref[k] = first[:, at]
            second_ref[k] = second[:, at]
        return 0

    lax.fori_loop(0, one_ref.shape[0] // 2, step, 0, unroll=2)


def close(sector, kept_ref, came_ref, out_hbm, done_ref, sems):
    size = kept_ref.shape[0] // 3
    moves = []
    for piece in range(3):
        at = slice(piece * size, (piece + 1) * size)
        done_ref[at] = (kept_ref[at] + came_ref[at].astype(F32)).astype(BF16)
        moves.append(pltpu.make_async_copy(done_ref.at[at], out_hbm.at[at, sector], sems.at[piece]))
        moves[-1].start()
    for move in moves:
        move.wait()


def close_one(kept_ref, came_ref, out_hbm, done_ref, sems):
    close(1, kept_ref, came_ref, out_hbm, done_ref, sems)


def close_zero(kept_ref, came_ref, _, out_hbm, done_ref, sems):
    close(0, kept_ref, came_ref, out_hbm, done_ref, sems)


def body(site_tensor, operators, one_index, weights, comp_charge, one_charge, sector_size, coupling):
    ops = operators.shape[0]
    sds = jax.ShapeDtypeStruct
    column = jnp.concatenate([one_index.reshape(512, 128), site_tensor.reshape(16, 128)], axis=0)
    far = lax.all_gather(column, "zh", axis=0)
    coef = jnp.where(comp_charge[:, None] == one_charge[None, :], weights, jnp.zeros((), BF16))
    message = call(
        spread_kernel, sds((16, MESSAGE, 128), BF16), [VMEM, VMEM], VMEM, [pltpu.VMEM((64, 128), F32)]
    )(coef, far)
    near = lax.all_to_all(message, PLANE, 0, 0, tiled=True)
    rows = ops * 8
    mixed = sds((16, rows, 128), BF16)
    scratch = [pltpu.VMEM((1024, 128), F32), pltpu.VMEM((16 * rows, 128), F32)]
    flops = 2 * ops * 2 * 128**3
    half, wide, site = sds((ops, 128, 128), BF16), sds((ops, 128, 128), F32), sds((2, 128, 512), BF16)
    mixed_one = call(mix_one, mixed, [VMEM], VMEM, scratch)(near)
    landed_one = lax.all_to_all(mixed_one, PLANE, 0, 0, tiled=True)
    own = call(site_kernel, site, [SMEM, SMEM, VMEM], VMEM)(coupling, sector_size, near)
    mixed_zero = call(mix_zero, mixed, [VMEM], VMEM, scratch)(near)
    zero, one = operators[:, 0], operators[:, 1]
    landed_zero = lax.all_to_all(mixed_zero, PLANE, 0, 0, tiled=True)
    upper = shift(own, -1)
    few = sds((4, 128, 128), BF16)
    pool, early, last = call(pool_kernel, [sds((4, 128, 512), BF16), few, few], [VMEM] * 2, [VMEM] * 3)(own, upper)
    leave, comb_one = call(front_kernel, [half, half], [SMEM] + [VMEM] * 3, [VMEM] * 2, flops=flops)(
        comp_charge, landed_one, one, early
    )
    came_one = shift(leave, 1)
    toward, again = call(
        middle_kernel,
        [wide, sds((4, 128, 512), BF16)],
        [SMEM] + [VMEM] * 2,
        [VMEM] * 2,
        [pltpu.VMEM((128, 256), BF16)],
        flops=2 * flops,
    )(comp_charge, comb_one, pool)
    leave, comb_zero = call(last_kernel, [half, half], [SMEM] + [VMEM] * 4, [VMEM] * 2, flops=flops)(
        comp_charge, landed_zero, zero, toward, last
    )
    came_zero = shift(leave, 1)
    first, second = call(
        own_kernel, [wide, wide], [SMEM] + [VMEM] * 3, [VMEM] * 2, [pltpu.VMEM((128, 512), BF16)], flops=4 * flops
    )(comp_charge, comb_one, comb_zero, again)
    whole = sds((ops, 2, 128, 128), BF16)
    scratch = [pltpu.VMEM((ops, 128, 128), BF16), DMA((3,))]
    out = call(close_one, whole, [VMEM] * 2, HBM, scratch)(second, came_one)
    return call(close_zero, whole, [VMEM, VMEM, HBM], HBM, scratch, input_output_aliases={2: 0})(first, came_zero, out)


def solution(mesh):
    fine = Mesh(mesh.devices.reshape(4, 4, 4, 4, 2), ("x", "y", "zh", "zl", "core"))
    pair, sector = ("x", "y", "zh"), ("zl", "core")
    return jax.shard_map(
        body,
        mesh=fine,
        in_specs=(
            P(None, sector, pair, None),
            P(pair, sector, None, None),
            P(pair, sector, None, None),
            P(pair, None),
            P(pair),
            P(),
            P(),
            P(),
        ),
        out_specs=P(pair, sector, None, None),
        check_vma=False,
    )
```

profile of v0, /device:TPU:1, one launch (start us, length us, event | category | flops | bytes accessed | tf_op | source)
XLA Modules:
  0.0 109.7 jit_solution(7183364530073146427)
XLA Ops:
  0.0 0.9 pad_maximum_fusion
  0.9 31.7 %all-gather = bf16[2112,128]{1,0:T(8,128)(2,1)S(1)} all-gather(bf16[528,128]{1,0:T(8,128)(2,1)S(1)} %pad_maximum_fusion), channel_id=2, replica_groups=mesh['x'=4,'y'=4,'zh'=4,'zl'=4,'core'=2] {'zh'}, dimensions={0}, use_global_device_ids=true | all-gather | bytes 675840 | tf_op jit(solution)/shard_map/all_gather | solution.py:243
  32.6 0.8 compare_select_fusion.c_ref
  33.4 0.1 shard_map.82
  33.5 17.3 %all_to_all.15.refs_0_.a_ref = bf16[16,224,128]{2,1,0:T(8,128)(2,1)S(1)} all-to-all(bf16[16,224,128]{2,1,0:T(8,128)(2,1)S(1)} %shard_map.82), channel_id=1, replica_groups=mesh['x'=4,'y'=4,'zh'=4,'zl'=4,'core'=2] {'x','y'}, dimensions={0} | all-to-all | bytes 1835008 | tf_op jit(solution)/shard_map/all_to_all | solution.py:248
  50.9 1.5 %shard_map.83 = bf16[16,192,128]{2,1,0:T(8,128)(2,1)} custom-call(bf16[16,224,128]{2,1,0:T(8,128)(2,1)S(1)} %all_to_all.15.refs_0_.a_ref), custom_call_target="tpu_custom_call" | custom-call | bytes 4194304 | tf_op jit(solution)/shard_map/pallas_call | solution.py:254
  52.3 3.7 %all-to-all-start.1 = ((bf16[16,192,128]{2,1,0:T(8,128)(2,1)}), bf16[16,192,128]{2,1,0:T(8,128)(2,1)S(1)}, u32[]{:S(2)}, u32[]{:S(2)}) async-start(bf16[16,192,128]{2,1,0:T(8,128)(2,1)} %shard_map.83), calls=%async_computation.1 | async-start | bytes 1572864 | tf_op jit(solution)/shard_map/all_to_all | solution.py:255
  56.1 0.0 copy-start.8
  56.1 0.0 copy-start.3
  56.1 1.5 %shard_map.87 = bf16[16,192,128]{2,1,0:T(8,128)(2,1)} custom-call(bf16[16,224,128]{2,1,0:T(8,128)(2,1)S(1)} %all_to_all.15.refs_0_.a_ref), custom_call_target="tpu_custom_call" | custom-call | bytes 4194304 | tf_op jit(solution)/shard_map/pallas_call | solution.py:257
  57.6 8.8 %all-to-all-done.1.r_ref = bf16[16,192,128]{2,1,0:T(8,128)(2,1)S(1)} async-done(((bf16[16,192,128]{2,1,0:T(8,128)(2,1)}), bf16[16,192,128]{2,1,0:T(8,128)(2,1)S(1)}, u32[]{:S(2)}, u32[]{:S(2)}) %all-to-all-start.1) | async-done | bytes 786464 | tf_op jit(solution)/shard_map/all_to_all | solution.py:255
  66.4 3.6 %all-to-all-start.2 = ((bf16[16,192,128]{2,1,0:T(8,128)(2,1)}), bf16[16,192,128]{2,1,0:T(8,128)(2,1)S(1)}, u32[]{:S(2)}, u32[]{:S(2)}) async-start(bf16[16,192,128]{2,1,0:T(8,128)(2,1)} %shard_map.87), calls=%async_computation.2 | async-start | bytes 1572864 | tf_op jit(solution)/shard_map/all_to_all | solution.py:259
  70.0 0.0 copy-done.8
  70.1 0.1 copy.11.coupling_ref
  70.1 0.0 copy-done.3
  70.1 0.8 shard_map.84.own_ref
  70.9 0.0 copy-start.2
  70.9 9.2 %collective-permute-start = (bf16[2,128,512]{2,1,0:T(8,128)(2,1)S(1)}, bf16[2,128,512]{2,1,0:T(8,128)(2,1)S(1)}, u32[]{:S(2)}, u32[]{:S(2)}) collective-permute-start(bf16[2,128,512]{2,1,0:T(8,128)(2,1)S(1)} %shard_map.84.own_ref), channel_id=1, source_target_pairs={{1,0},{2,1},{3,2},{4,3},{5,4},{6,5},{7,6},{9,8},{10,9},{11,10},{12... | collective-permute-start | bytes 786440 | tf_op jit(solution)/shard_map/ppermute | solution.py:35
  80.1 1.5 %slice_bitcast_fusion = (bf16[24,128,128]{2,1,0:T(8,128)(2,1)S(1)}, bf16[24,128,128]{2,1,0:T(8,128)(2,1)S(1)}) fusion(bf16[24,2,128,128]{3,2,1,0:T(8,128)(2,1)} %param.9), kind=kLoop, calls=%fused_computation | loop fusion | bytes 3145728 | tf_op jit(solution)/shard_map/squeeze | solution.py:258
  81.6 2.9 %collective-permute-done.up_ref = bf16[2,128,512]{2,1,0:T(8,128)(2,1)S(1)} collective-permute-done((bf16[2,128,512]{2,1,0:T(8,128)(2,1)S(1)}, bf16[2,128,512]{2,1,0:T(8,128)(2,1)S(1)}, u32[]{:S(2)}, u32[]{:S(2)}) %collective-permute-start) | collective-permute-done | bytes 262176 | tf_op jit(solution)/shard_map/ppermute | solution.py:35
  84.6 0.1 shard_map.85
  84.7 0.0 copy-done.2
  84.7 1.3 %shard_map.86 = (bf16[24,128,128]{2,1,0:T(8,128)(2,1)S(1)}, bf16[24,128,128]{2,1,0:T(8,128)(2,1)S(1)}) custom-call(s32[24]{0:T(128)S(1)} %copy-done.2, bf16[16,192,128]{2,1,0:T(8,128)(2,1)S(1)} %all-to-all-done.1.r_ref, bf16[24,128,128]{2,1,0:T(8,128)(2,1)S(1)} %get-tuple-element.28.op_ref, bf16[4,128,128]{2,1,0:T(8,128)(2,1)S(1)} %get-tuple-element.16.early_ref), custom_call_target="tpu_custom_call" | custom-call | flops 201326592 | bytes 4194304 | tf_op jit(solution)/shard_map/pallas_call | solution.py:263
  85.9 1.9 %collective-permute-start.2 = (bf16[24,128,128]{2,1,0:T(8,128)(2,1)S(1)}, bf16[24,128,128]{2,1,0:T(8,128)(2,1)S(1)}, u32[]{:S(2)}, u32[]{:S(2)}) collective-permute-start(bf16[24,128,128]{2,1,0:T(8,128)(2,1)S(1)} %get-tuple-element.26), channel_id=1, source_target_pairs={{0,1},{1,2},{2,3},{3,4},{4,5},{5,6},{6,7},{8,9},{9,10},{10,11},{11... | collective-permute-start | bytes 2359304 | tf_op jit(solution)/shard_map/ppermute | solution.py:35
  87.9 3.3 %shard_map.88 = (f32[24,128,128]{2,1,0:T(8,128)S(1)}, bf16[4,128,512]{2,1,0:T(8,128)(2,1)S(1)}) custom-call(s32[24]{0:T(128)S(1)} %copy-done.2, bf16[24,128,128]{2,1,0:T(8,128)(2,1)S(1)} %get-tuple-element.17.comb_ref.one_ref, bf16[4,128,512]{2,1,0:T(8,128)(2,1)S(1)} %get-tuple-element.18.pool_ref), custom_call_target="tpu_custom_call" | custom-call | flops 402653184 | bytes 4194304 | tf_op jit(solution)/shard_map/pallas_call | solution.py:267
  91.2 0.0 copy-start
  91.2 1.1 %copy-done = f32[24,128,128]{2,1,0:T(8,128)} copy-done((f32[24,128,128]{2,1,0:T(8,128)}, f32[24,128,128]{2,1,0:T(8,128)S(1)}, u32[]{:S(2)}) %copy-start) | copy-done | bytes 1572888
  92.3 0.0 copy-start.4
  92.3 0.9 copy-done.4
  93.2 0.0 copy-start.6
  93.2 0.8 copy-done.6
  94.0 0.0 all-to-all-done.2.r_ref
  94.0 0.0 copy-start.1
  94.0 1.4 %copy-done.1 = f32[24,128,128]{2,1,0:T(8,128)S(1)} copy-done((f32[24,128,128]{2,1,0:T(8,128)S(1)}, f32[24,128,128]{2,1,0:T(8,128)}, u32[]{:S(2)}) %copy-start.1) | copy-done | bytes 1572888
  95.5 0.0 copy-start.5
  95.5 0.0 copy-start.7
  95.5 1.3 %shard_map.89 = (bf16[24,128,128]{2,1,0:T(8,128)(2,1)S(1)}, bf16[24,128,128]{2,1,0:T(8,128)(2,1)S(1)}) custom-call(s32[24]{0:T(128)S(1)} %copy-done.2, bf16[16,192,128]{2,1,0:T(8,128)(2,1)S(1)} %all-to-all-done.2.r_ref, bf16[24,128,128]{2,1,0:T(8,128)(2,1)S(1)} %get-tuple-element.27.op_ref, f32[24,128,128]{2,1,0:T(8,128)S(1)} %copy-done.1, ...), custom_call_target="tpu_custom_call" | custom-call | flops 201326592 | bytes 4194304 | tf_op jit(solution)/shard_map/pallas_call | solution.py:275
  96.7 3.1 %collective-permute-start.1 = (bf16[24,128,128]{2,1,0:T(8,128)(2,1)S(1)}, bf16[24,128,128]{2,1,0:T(8,128)(2,1)S(1)}, u32[]{:S(2)}, u32[]{:S(2)}) collective-permute-start(bf16[24,128,128]{2,1,0:T(8,128)(2,1)S(1)} %get-tuple-element.24), channel_id=1, source_target_pairs={{0,1},{1,2},{2,3},{3,4},{4,5},{5,6},{6,7},{8,9},{9,10},{10,11},{11... | collective-permute-start | bytes 2359304 | tf_op jit(solution)/shard_map/ppermute | solution.py:35
  99.8 0.0 copy-done.5
  99.9 0.0 copy-done.7
  99.9 4.6 %shard_map.90 = (f32[24,128,128]{2,1,0:T(8,128)S(1)}, f32[24,128,128]{2,1,0:T(8,128)S(1)}) custom-call(s32[24]{0:T(128)S(1)} %copy-done.2, bf16[24,128,128]{2,1,0:T(8,128)(2,1)S(1)} %copy-done.5, bf16[24,128,128]{2,1,0:T(8,128)(2,1)S(1)} %get-tuple-element.21.zero_ref, bf16[4,128,512]{2,1,0:T(8,128)(2,1)S(1)} %copy-done.7), custom_call_target="tpu_custom_call" | custom-call | flops 805306368 | bytes 4194304 | tf_op jit(solution)/shard_map/pallas_call | solution.py:279
  104.4 0.0 collective-permute-done.2.came_ref
  104.4 0.9 shard_map.91._
  105.4 3.4 %collective-permute-done.1.came_ref = bf16[24,128,128]{2,1,0:T(8,128)(2,1)S(1)} collective-permute-done((bf16[24,128,128]{2,1,0:T(8,128)(2,1)S(1)}, bf16[24,128,128]{2,1,0:T(8,128)(2,1)S(1)}, u32[]{:S(2)}, u32[]{:S(2)}) %collective-permute-start.1) | collective-permute-done | bytes 786464 | tf_op jit(solution)/shard_map/ppermute | solution.py:35
  108.8 1.0 shard_map.92
Async XLA Ops:
  52.3 14.1 %all-to-all-start.1 = ((bf16[16,192,128]{2,1,0:T(8,128)(2,1)}), bf16[16,192,128]{2,1,0:T(8,128)(2,1)S(1)}, u32[]{:S(2)}, u32[]{:S(2)}) async-start(bf16[16,192,128]{2,1,0:T(8,128)(2,1)} %shard_map.83), calls=%async_computation.1 | async-start | bytes 1572864 | tf_op jit(solution)/shard_map/all_to_all | solution.py:255
  56.1 14.0 %copy-start.8 = (s32[16,4]{0,1:T(4,128)S(1)}, s32[16,4]{0,1:T(4,128)}, u32[]{:S(2)}) copy-start(s32[16,4]{0,1:T(4,128)} %param.15) | copy-start | bytes 772
  56.1 14.1 %copy-start.3 = (s32[16]{0:T(128)S(1)}, s32[16]{0:T(128)}, u32[]{:S(2)}) copy-start(s32[16]{0:T(128)} %size_ref.1) | copy-start | bytes 196
  66.4 27.6 %all-to-all-start.2 = ((bf16[16,192,128]{2,1,0:T(8,128)(2,1)}), bf16[16,192,128]{2,1,0:T(8,128)(2,1)S(1)}, u32[]{:S(2)}, u32[]{:S(2)}) async-start(bf16[16,192,128]{2,1,0:T(8,128)(2,1)} %shard_map.87), calls=%async_computation.2 | async-start | bytes 1572864 | tf_op jit(solution)/shard_map/all_to_all | solution.py:259
  70.9 13.8 %copy-start.2 = (s32[24]{0:T(128)S(1)}, s32[24]{0:T(128)}, u32[]{:S(2)}) copy-start(s32[24]{0:T(128)} %charge_ref.7) | copy-start | bytes 292
  70.9 13.6 %collective-permute-start = (bf16[2,128,512]{2,1,0:T(8,128)(2,1)S(1)}, bf16[2,128,512]{2,1,0:T(8,128)(2,1)S(1)}, u32[]{:S(2)}, u32[]{:S(2)}) collective-permute-start(bf16[2,128,512]{2,1,0:T(8,128)(2,1)S(1)} %shard_map.84.own_ref), channel_id=1, source_target_pairs={{1,0},{2,1},{3,2},{4,3},{5,4},{6,5},{7,6},{9,8},{10,9},{11,10},{12... | collective-permute-start | bytes 786440 | tf_op jit(solution)/shard_map/ppermute | solution.py:35
  85.9 18.5 %collective-permute-start.2 = (bf16[24,128,128]{2,1,0:T(8,128)(2,1)S(1)}, bf16[24,128,128]{2,1,0:T(8,128)(2,1)S(1)}, u32[]{:S(2)}, u32[]{:S(2)}) collective-permute-start(bf16[24,128,128]{2,1,0:T(8,128)(2,1)S(1)} %get-tuple-element.26), channel_id=1, source_target_pairs={{0,1},{1,2},{2,3},{3,4},{4,5},{5,6},{6,7},{8,9},{9,10},{10,11},{11... | collective-permute-start | bytes 2359304 | tf_op jit(solution)/shard_map/ppermute | solution.py:35
  91.2 1.1 %copy-start = (f32[24,128,128]{2,1,0:T(8,128)}, f32[24,128,128]{2,1,0:T(8,128)S(1)}, u32[]{:S(2)}) copy-start(f32[24,128,128]{2,1,0:T(8,128)S(1)} %get-tuple-element.19.next_ref) | copy-start | bytes 4718596
  92.3 0.9 copy-start.4
  93.2 0.8 copy-start.6
  94.0 1.4 %copy-start.1 = (f32[24,128,128]{2,1,0:T(8,128)S(1)}, f32[24,128,128]{2,1,0:T(8,128)}, u32[]{:S(2)}) copy-start(f32[24,128,128]{2,1,0:T(8,128)} %copy-done) | copy-start | bytes 4718596
  95.5 4.4 %copy-start.5 = (bf16[24,128,128]{2,1,0:T(8,128)(2,1)S(1)}, bf16[24,128,128]{2,1,0:T(8,128)(2,1)}, u32[]{:S(2)}) copy-start(bf16[24,128,128]{2,1,0:T(8,128)(2,1)} %copy-done.4) | copy-start | bytes 2359300
  95.5 4.4 %copy-start.7 = (bf16[4,128,512]{2,1,0:T(8,128)(2,1)S(1)}, bf16[4,128,512]{2,1,0:T(8,128)(2,1)}, u32[]{:S(2)}) copy-start(bf16[4,128,512]{2,1,0:T(8,128)(2,1)} %copy-done.6) | copy-start | bytes 1572868
  96.7 12.0 %collective-permute-start.1 = (bf16[24,128,128]{2,1,0:T(8,128)(2,1)S(1)}, bf16[24,128,128]{2,1,0:T(8,128)(2,1)S(1)}, u32[]{:S(2)}, u32[]{:S(2)}) collective-permute-start(bf16[24,128,128]{2,1,0:T(8,128)(2,1)S(1)} %get-tuple-element.24), channel_id=1, source_target_pairs={{0,1},{1,2},{2,3},{3,4},{4,5},{5,6},{6,7},{8,9},{9,10},{10,11},{11... | collective-permute-start | bytes 2359304 | tf_op jit(solution)/shard_map/ppermute | solution.py:35
where the time goes:
time: 110 us
  blocking collectives  49 us (45%)
  starting transfers between devices  21.5 us (20%)
  Pallas kernels  16.3 us (15%)
  waiting for transfers between devices  15.1 us (14%)
  local copies, waits for them, and re-layouts  5.87 us (5%)
  other arithmetic  1.71 us (2%)
    all_gather x1, blocking collectives, body(): far = lax.all_gather(column, 'zh', axis=0)  31.7 us
    all_to_all x1, blocking collectives, body(): near = lax.all_to_all(message, PLANE, 0, 0, tiled=True)  17.3 us
    ppermute x3, starting transfers between devices, shift(): lax.ppermute(value, GROUP, [(a, a + steps) for a in range(first, last)])  14.2 us
    all_to_all x1, waiting for transfers between devices, body(): landed_one = lax.all_to_all(mixed_one, PLANE, 0, 0, tiled=True)  8.83 us
    ppermute x3, waiting for transfers between devices, shift(): lax.ppermute(value, GROUP, [(a, a + steps) for a in range(first, last)])  6.3 us
    pallas_call x1, Pallas kernels, body(): call(own_kernel, [wide, wide], [SMEM] + [VMEM] * 3, [VMEM] * 2, [pltpu.VM...  4.55 us
    unnamed x19, local copies, waits for them, and re-layouts  4.35 us
    all_to_all x1, starting transfers between devices, body(): landed_one = lax.all_to_all(mixed_one, PLANE, 0, 0, tiled=True)  3.72 us
  transfers between devices with their start and end apart: 5, of which 3 were waited for; matrix products, arithmetic and copies ran while one was open for 1% of the time, Pallas kernels for 12%

commit v1 on v0

--- a/solution.py
+++ b/solution.py
@@ -57,29 +57,28 @@
         out_ref[d, SITE_AT:, :] = site
 
 
-def mix(half, a_ref, out_ref, gf_ref, cf_ref):
-    planes, rows = out_ref.shape[:2]
+def mix_kernel(a_ref, out_hbm, gf_ref, cf_ref, out_ref, sems):
+    planes, rows = out_ref.shape[0], out_ref.shape[1] // 2
     ops = rows // 8
     coef = a_ref[:, COEF_AT : COEF_AT + ops, :].astype(F32).reshape(planes * ops, 128).astype(BF16)
-    gf_ref[...] = a_ref[:, half * 64 : half * 64 + 64, :].astype(F32).reshape(1024, 128)
-    for r in range(8):
-        block = gf_ref[pl.ds(r, 128, stride=8), :].astype(BF16)
-        cf_ref[pl.ds(r, planes * ops, stride=8), :] = jnp.dot(coef, block, preferred_element_type=F32)
-
-    def finish(d, _):
-        at = pl.multiple_of(d * rows, 16)
-        out_ref[d] = cf_ref[pl.ds(at, rows), :].astype(BF16)
-        return 0
-
-    lax.fori_loop(0, planes, finish, 0, unroll=4)
-
-
-def mix_one(*refs):
-    mix(0, *refs)
-
-
-def mix_zero(*refs):
-    mix(1, *refs)
+    moves = []
+    for half in range(2):
+        gf_ref[half] = a_ref[:, half * 64 : half * 64 + 64, :].astype(F32).reshape(1024, 128)
+        for r in range(8):
+            block = gf_ref[half, pl.ds(r, 128, stride=8), :].astype(BF16)
+            cf_ref[half, pl.ds(r, planes * ops, stride=8), :] = jnp.dot(coef, block, preferred_element_type=F32)
+
+        def finish(d, _, half=half):
+            at = pl.multiple_of(d * rows, 16)
+            out_ref[d, half * rows : (half + 1) * rows, :] = cf_ref[half, pl.ds(at, rows), :].astype(BF16)
+            return 0
+
+        lax.fori_loop(0, planes, finish, 0, unroll=4)
+        at = slice(half * rows, (half + 1) * rows)
+        moves.append(pltpu.make_async_copy(out_ref.at[:, at], out_hbm.at[:, at], sems.at[half]))
+        moves[-1].start()
+    for move in moves:
+        move.wait()
 
 
 def state_order(coupling_ref):
@@ -107,12 +106,13 @@
             own_ref[s, :, n * 128 : (n + 1) * 128] = block.astype(BF16)
 
 
-def combine(r_ref, own, h):
-    both = r_ref[:, pl.ds(pl.multiple_of(h * 16, 16), 16), :].astype(F32)
+def combine(r_ref, op_ref, h, sector):
+    base = (1 - sector) * (r_ref.shape[1] // 2)
+    both = r_ref[:, pl.ds(pl.multiple_of(base + h * 16, 16), 16), :].astype(F32)
     pair = []
     for e in range(2):
         summed = both[:, e * 8 : (e + 1) * 8, :].reshape(128, 128)
-        pair.append((own[e].astype(F32) + summed).astype(BF16))
+        pair.append((op_ref[2 * h + e].astype(F32) + summed).astype(BF16))
     return pair
 
 
@@ -138,21 +138,18 @@
     return jnp.concatenate(blocks, axis=1).astype(BF16)
 
 
-def pool_kernel(own_ref, up_ref, pool_ref, early_ref, last_ref):
+def pool_kernel(own_ref, up_ref, pool_ref, early_ref):
     for s in range(2):
         pool_ref[s] = own_ref[s]
         pool_ref[2 + s] = up_ref[s]
         early_ref[1 + s] = up_ref[s, :, 384:]
-        last_ref[s] = own_ref[s, :, 384:]
     early_ref[0] = own_ref[1, :, 384:]
     early_ref[3] = turned(own_ref, 1, (3,))
-    last_ref[2] = up_ref[0, :, 384:]
-    last_ref[3] = turned(own_ref, 0, (3,))
 
 
 def front_kernel(charge_ref, r_ref, op_ref, early_ref, out_ref, comb_ref):
     def step(h, _):
-        pair = combine(r_ref, [op_ref[2 * h + e] for e in range(2)], h)
+        pair = combine(r_ref, op_ref, h, 1)
         parts = []
         for e in range(2):
             comb_ref[2 * h + e] = pair[e]
@@ -165,34 +162,25 @@
     lax.fori_loop(0, op_ref.shape[0] // 2, step, 0, unroll=12)
 
 
-def middle_kernel(charge_ref, comb_ref, pool_ref, next_ref, again_ref, left_ref):
-    again_ref[...] = pool_ref[...]
-    left_ref[...] = turned(pool_ref, 1, (1, 2))
+def last_kernel(charge_ref, r_ref, op_ref, one_ref, pool_ref, out_ref, comb_ref, left_ref):
+    left_ref[...] = jnp.concatenate([turned(pool_ref, 1, (1, 2)), turned(pool_ref, 0, (3,))], axis=1)
 
     def step(h, _):
-        parts = [inner(comb_ref[2 * h + e], pool_ref[charge_ref[2 * h + e] + 1, :, 128:384]) for e in range(2)]
-        one = product(left_ref[...], stacked(parts, 0))
-        for e in range(2):
-            next_ref[2 * h + e] = one[:, e * 128 : (e + 1) * 128]
+        pair = combine(r_ref, op_ref, h, 0)
+        tall = []
+        for e in range(2):
+            k = 2 * h + e
+            q = charge_ref[k]
+            comb_ref[k] = pair[e]
+            ones = inner(one_ref[k], pool_ref[q + 1, :, 128:384])
+            two = inner(pair[e], pool_ref[q, :, 384:])
+            tall.append(jnp.concatenate([ones[:, :128], ones[:, 128:], two], axis=0))
+        total = product(left_ref[...], jnp.concatenate(tall, axis=1))
+        for e in range(2):
+            out_ref[2 * h + e] = total[:, e * 128 : (e + 1) * 128].astype(BF16)
         return 0
 
-    lax.fori_loop(0, comb_ref.shape[0] // 2, step, 0, unroll=6)
-
-
-def last_kernel(charge_ref, r_ref, op_ref, next_ref, last_ref, out_ref, comb_ref):
-    def step(h, _):
-        pair = combine(r_ref, [op_ref[2 * h + e] for e in range(2)], h)
-        parts = []
-        for e in range(2):
-            comb_ref[2 * h + e] = pair[e]
-            parts.append(inner(pair[e], last_ref[charge_ref[2 * h + e]]))
-        two = product(last_ref[3], joined(parts, 0, 128))
-        for e in range(2):
-            k = 2 * h + e
-            out_ref[k] = (two[:, e * 128 : (e + 1) * 128] + next_ref[k]).astype(BF16)
-        return 0
-
-    lax.fori_loop(0, op_ref.shape[0] // 2, step, 0, unroll=12)
+    lax.fori_loop(0, one_ref.shape[0] // 2, step, 0, unroll=6)
 
 
 def own_kernel(charge_ref, one_ref, zero_ref, pool_ref, first_ref, second_ref, left_ref):
@@ -247,38 +235,34 @@
     )(coef, far)
     near = lax.all_to_all(message, PLANE, 0, 0, tiled=True)
     rows = ops * 8
-    mixed = sds((16, rows, 128), BF16)
-    scratch = [pltpu.VMEM((1024, 128), F32), pltpu.VMEM((16 * rows, 128), F32)]
+    scratch = [pltpu.VMEM((2, 1024, 128), F32), pltpu.VMEM((2, 16 * rows, 128), F32)]
     flops = 2 * ops * 2 * 128**3
     half, wide, site = sds((ops, 128, 128), BF16), sds((ops, 128, 128), F32), sds((2, 128, 512), BF16)
-    mixed_one = call(mix_one, mixed, [VMEM], VMEM, scratch)(near)
-    landed_one = lax.all_to_all(mixed_one, PLANE, 0, 0, tiled=True)
+    mixed = call(
+        mix_kernel,
+        pltpu.HBM((16, 2 * rows, 128), BF16),
+        [VMEM],
+        HBM,
+        scratch + [pltpu.VMEM((16, 2 * rows, 128), BF16), DMA((2,))],
+    )(near)
+    landed = lax.all_to_all(mixed, PLANE, 0, 0, tiled=True)
     own = call(site_kernel, site, [SMEM, SMEM, VMEM], VMEM)(coupling, sector_size, near)
-    mixed_zero = call(mix_zero, mixed, [VMEM], VMEM, scratch)(near)
+    upper = shift(own, -1)
+    pool, early = call(
+        pool_kernel, [sds((4, 128, 512), BF16), sds((4, 128, 128), BF16)], [VMEM] * 2, [VMEM] * 2
+    )(own, upper)
     zero, one = operators[:, 0], operators[:, 1]
-    landed_zero = lax.all_to_all(mixed_zero, PLANE, 0, 0, tiled=True)
-    upper = shift(own, -1)
-    few = sds((4, 128, 128), BF16)
-    pool, early, last = call(pool_kernel, [sds((4, 128, 512), BF16), few, few], [VMEM] * 2, [VMEM] * 3)(own, upper)
     leave, comb_one = call(front_kernel, [half, half], [SMEM] + [VMEM] * 3, [VMEM] * 2, flops=flops)(
-        comp_charge, landed_one, one, early
+        comp_charge, landed, one, early
     )
     came_one = shift(leave, 1)
-    toward, again = call(
-        middle_kernel,
-        [wide, sds((4, 128, 512), BF16)],
-        [SMEM] + [VMEM] * 2,
-        [VMEM] * 2,
-        [pltpu.VMEM((128, 256), BF16)],
-        flops=2 * flops,
-    )(comp_charge, comb_one, pool)
-    leave, comb_zero = call(last_kernel, [half, half], [SMEM] + [VMEM] * 4, [VMEM] * 2, flops=flops)(
-        comp_charge, landed_zero, zero, toward, last
-    )
+    leave, comb_zero = call(
+        last_kernel, [half, half], [SMEM] + [VMEM] * 4, [VMEM] * 2, [pltpu.VMEM((128, 384), BF16)], flops=3 * flops
+    )(comp_charge, landed, zero, comb_one, pool)
     came_zero = shift(leave, 1)
     first, second = call(
         own_kernel, [wide, wide], [SMEM] + [VMEM] * 3, [VMEM] * 2, [pltpu.VMEM((128, 512), BF16)], flops=4 * flops
-    )(comp_charge, comb_one, comb_zero, again)
+    )(comp_charge, comb_one, comb_zero, pool)
     whole = sds((ops, 2, 128, 128), BF16)
     scratch = [pltpu.VMEM((ops, 128, 128), BF16), DMA((3,))]
     out = call(close_one, whole, [VMEM] * 2, HBM, scratch)(second, came_one)

time: 110 us -> 105 us (0.955)
  starting transfers between devices: 21.5 us -> 26.8 us
  waiting for transfers between devices: 15.1 us -> 11 us
  local copies, waits for them, and re-layouts: 5.87 us -> 2.38 us
  Pallas kernels: 16.3 us -> 13.9 us
    ppermute x3, starting transfers between devices: 14.2 us -> 23.1 us  [shift(): lax.ppermute(value, GROUP, [(a, a + steps) for a in range(first, last)])]
    all_to_all x2 -> x1, waiting for transfers between devices: 8.83 us -> 1.31 us  [body(): landed = lax.all_to_all(mixed, PLANE, 0, 0, tiled=True)]
    all_to_all x2 -> x1, starting transfers between devices: 7.33 us -> 3.74 us  [body(): landed = lax.all_to_all(mixed, PLANE, 0, 0, tiled=True)]
    unnamed x19 -> x11, local copies, waits for them, and re-layouts: 4.35 us -> 0.9 us
    ppermute x3, waiting for transfers between devices: 6.3 us -> 9.66 us  [shift(): lax.ppermute(value, GROUP, [(a, a + steps) for a in range(first, last)])]
    pallas_call x5 -> x3, Pallas kernels: 7.66 us -> 5.37 us  [the longest x1 3.23 us: body(): call(last_kernel, [half, half], [SMEM] + [VMEM] * 4, [VMEM] * 2, [pltpu.V...]
  transfers between devices with their start and end apart: 5 -> 4, of which waited for: 3 -> 3; matrix products, arithmetic and copies ran while one was open for 1% -> 1% of each run, Pallas kernels for 12% -> 9%
where the time goes in v1:
time: 105 us
  blocking collectives  49 us (47%)
  starting transfers between devices  26.8 us (26%)
  Pallas kernels  13.9 us (13%)
  waiting for transfers between devices  11 us (10%)
  local copies, waits for them, and re-layouts  2.38 us (2%)
  other arithmetic  1.71 us (2%)
    all_gather x1, blocking collectives, body(): far = lax.all_gather(column, 'zh', axis=0)  31.7 us
    ppermute x3, starting transfers between devices, shift(): lax.ppermute(value, GROUP, [(a, a + steps) for a in range(first, last)])  23.1 us
    all_to_all x1, blocking collectives, body(): near = lax.all_to_all(message, PLANE, 0, 0, tiled=True)  17.3 us
    ppermute x3, waiting for transfers between devices, shift(): lax.ppermute(value, GROUP, [(a, a + steps) for a in range(first, last)])  9.66 us
    pallas_call x1, Pallas kernels, body(): call(own_kernel, [wide, wide], [SMEM] + [VMEM] * 3, [VMEM] * 2, [pltpu.VM...  4.5 us
    all_to_all x1, starting transfers between devices, body(): landed = lax.all_to_all(mixed, PLANE, 0, 0, tiled=True)  3.74 us
    pallas_call x1, Pallas kernels, body(): call(last_kernel, [half, half], [SMEM] + [VMEM] * 4, [VMEM] * 2, [pltpu.V...  3.23 us
  transfers between devices with their start and end apart: 4, of which 3 were waited for; matrix products, arithmetic and copies ran while one was open for 1% of the time, Pallas kernels for 9%

profile of v1, /device:TPU:1, one launch (start us, length us, event | category | flops | bytes accessed | tf_op | source)
XLA Modules:
  0.0 104.9 jit_solution(15367701768972145641)
XLA Ops:
  0.0 0.9 pad_maximum_fusion
  0.9 31.7 %all-gather = bf16[2112,128]{1,0:T(8,128)(2,1)S(1)} all-gather(bf16[528,128]{1,0:T(8,128)(2,1)S(1)} %pad_maximum_fusion), channel_id=2, replica_groups=mesh['x'=4,'y'=4,'zh'=4,'zl'=4,'core'=2] {'zh'}, dimensions={0}, use_global_device_ids=true | all-gather | bytes 675840 | tf_op jit(solution)/shard_map/all_gather | solution.py:231
  32.6 0.8 compare_select_fusion.c_ref
  33.4 0.1 shard_map.82
  33.5 17.3 %all_to_all.10.a_ref = bf16[16,224,128]{2,1,0:T(8,128)(2,1)S(1)} all-to-all(bf16[16,224,128]{2,1,0:T(8,128)(2,1)S(1)} %shard_map.82), channel_id=1, replica_groups=mesh['x'=4,'y'=4,'zh'=4,'zl'=4,'core'=2] {'x','y'}, dimensions={0} | all-to-all | bytes 1835008 | tf_op jit(solution)/shard_map/all_to_all | solution.py:236
  50.9 2.0 %shard_map.83 = bf16[16,384,128]{2,1,0:T(8,128)(2,1)} custom-call(bf16[16,224,128]{2,1,0:T(8,128)(2,1)S(1)} %all_to_all.10.a_ref), custom_call_target="tpu_custom_call" | custom-call | bytes 4194304 | tf_op jit(solution)/shard_map/pallas_call | solution.py:241
  52.9 0.0 copy-start.4
  52.9 0.0 copy-start.3
  52.9 3.7 %all-to-all-start.1 = ((bf16[16,384,128]{2,1,0:T(8,128)(2,1)}), bf16[16,384,128]{2,1,0:T(8,128)(2,1)S(1)}, u32[]{:S(2)}, u32[]{:S(2)}) async-start(bf16[16,384,128]{2,1,0:T(8,128)(2,1)} %shard_map.83), calls=%async_computation.1 | async-start | bytes 3145728 | tf_op jit(solution)/shard_map/all_to_all | solution.py:248
  56.7 0.0 copy-done.4
  56.7 0.1 copy.11.coupling_ref
  56.8 0.0 copy-done.3
  56.8 0.8 shard_map.84.own_ref
  57.5 0.0 copy-start.2
  57.5 8.0 %collective-permute-start = (bf16[2,128,512]{2,1,0:T(8,128)(2,1)S(1)}, bf16[2,128,512]{2,1,0:T(8,128)(2,1)S(1)}, u32[]{:S(2)}, u32[]{:S(2)}) collective-permute-start(bf16[2,128,512]{2,1,0:T(8,128)(2,1)S(1)} %shard_map.84.own_ref), channel_id=1, source_target_pairs={{1,0},{2,1},{3,2},{4,3},{5,4},{6,5},{7,6},{9,8},{10,9},{11,10},{12... | collective-permute-start | bytes 786440 | tf_op jit(solution)/shard_map/ppermute | solution.py:35
  65.6 1.5 %slice_bitcast_fusion = (bf16[24,128,128]{2,1,0:T(8,128)(2,1)S(1)}, bf16[24,128,128]{2,1,0:T(8,128)(2,1)S(1)}) fusion(bf16[24,2,128,128]{3,2,1,0:T(8,128)(2,1)} %param.9), kind=kLoop, calls=%fused_computation | loop fusion | bytes 3145728 | tf_op jit(solution)/shard_map/squeeze | solution.py:254
  67.1 3.0 %collective-permute-done.up_ref = bf16[2,128,512]{2,1,0:T(8,128)(2,1)S(1)} collective-permute-done((bf16[2,128,512]{2,1,0:T(8,128)(2,1)S(1)}, bf16[2,128,512]{2,1,0:T(8,128)(2,1)S(1)}, u32[]{:S(2)}, u32[]{:S(2)}) %collective-permute-start) | collective-permute-done | bytes 262176 | tf_op jit(solution)/shard_map/ppermute | solution.py:35
  70.0 0.1 shard_map.85
  70.2 0.0 copy-start
  70.2 0.8 copy-done
  71.0 1.3 %all-to-all-done.1.r_ref = bf16[16,384,128]{2,1,0:T(8,128)(2,1)S(1)} async-done(((bf16[16,384,128]{2,1,0:T(8,128)(2,1)}), bf16[16,384,128]{2,1,0:T(8,128)(2,1)S(1)}, u32[]{:S(2)}, u32[]{:S(2)}) %all-to-all-start.1) | async-done | bytes 1572896 | tf_op jit(solution)/shard_map/all_to_all | solution.py:248
  72.3 0.0 copy-start.1
  72.3 0.0 copy-done.2
  72.3 1.2 %shard_map.86 = (bf16[24,128,128]{2,1,0:T(8,128)(2,1)S(1)}, bf16[24,128,128]{2,1,0:T(8,128)(2,1)S(1)}) custom-call(s32[24]{0:T(128)S(1)} %copy-done.2, bf16[16,384,128]{2,1,0:T(8,128)(2,1)S(1)} %all-to-all-done.1.r_ref, bf16[24,128,128]{2,1,0:T(8,128)(2,1)S(1)} %get-tuple-element.22.op_ref, bf16[4,128,128]{2,1,0:T(8,128)(2,1)S(1)} %get-tuple-element.13.early_ref), custom_call_target="tpu_custom_call" | custom-call | flops 201326592 | bytes 4194304 | tf_op jit(solution)/shard_map/pallas_call | solution.py:255
  73.5 13.1 %collective-permute-start.2 = (bf16[24,128,128]{2,1,0:T(8,128)(2,1)S(1)}, bf16[24,128,128]{2,1,0:T(8,128)(2,1)S(1)}, u32[]{:S(2)}, u32[]{:S(2)}) collective-permute-start(bf16[24,128,128]{2,1,0:T(8,128)(2,1)S(1)} %get-tuple-element.20), channel_id=1, source_target_pairs={{0,1},{1,2},{2,3},{3,4},{4,5},{5,6},{6,7},{8,9},{9,10},{10,11},{11... | collective-permute-start | bytes 2359304 | tf_op jit(solution)/shard_map/ppermute | solution.py:35
  86.7 0.0 copy-done.1
  86.7 3.2 %shard_map.87 = (bf16[24,128,128]{2,1,0:T(8,128)(2,1)S(1)}, bf16[24,128,128]{2,1,0:T(8,128)(2,1)S(1)}) custom-call(s32[24]{0:T(128)S(1)} %copy-done.2, bf16[16,384,128]{2,1,0:T(8,128)(2,1)S(1)} %all-to-all-done.1.r_ref, bf16[24,128,128]{2,1,0:T(8,128)(2,1)S(1)} %get-tuple-element.21.op_ref, bf16[24,128,128]{2,1,0:T(8,128)(2,1)S(1)} %get-tuple-element.14.one_ref, ...), custom_call_target="tpu_custom_call" | custom-call | flops 603979776 | bytes 4194304 | tf_op jit(solution)/shard_map/pallas_call | solution.py:259
  89.9 1.9 %collective-permute-start.1 = (bf16[24,128,128]{2,1,0:T(8,128)(2,1)S(1)}, bf16[24,128,128]{2,1,0:T(8,128)(2,1)S(1)}, u32[]{:S(2)}, u32[]{:S(2)}) collective-permute-start(bf16[24,128,128]{2,1,0:T(8,128)(2,1)S(1)} %get-tuple-element.18), channel_id=1, source_target_pairs={{0,1},{1,2},{2,3},{3,4},{4,5},{5,6},{6,7},{8,9},{9,10},{10,11},{11... | collective-permute-start | bytes 2359304 | tf_op jit(solution)/shard_map/ppermute | solution.py:35
  91.8 4.5 %shard_map.88 = (f32[24,128,128]{2,1,0:T(8,128)S(1)}, f32[24,128,128]{2,1,0:T(8,128)S(1)}) custom-call(s32[24]{0:T(128)S(1)} %copy-done.2, bf16[24,128,128]{2,1,0:T(8,128)(2,1)S(1)} %get-tuple-element.14.one_ref, bf16[24,128,128]{2,1,0:T(8,128)(2,1)S(1)} %get-tuple-element.16.zero_ref, bf16[4,128,512]{2,1,0:T(8,128)(2,1)S(1)} %copy-done.1), custom_call_target="tpu_custom_call" | custom-call | flops 805306368 | bytes 4194304 | tf_op jit(solution)/shard_map/pallas_call | solution.py:263
  96.3 0.0 collective-permute-done.2.came_ref
  96.4 0.9 shard_map.89._
  97.3 6.7 %collective-permute-done.1.came_ref = bf16[24,128,128]{2,1,0:T(8,128)(2,1)S(1)} collective-permute-done((bf16[24,128,128]{2,1,0:T(8,128)(2,1)S(1)}, bf16[24,128,128]{2,1,0:T(8,128)(2,1)S(1)}, u32[]{:S(2)}, u32[]{:S(2)}) %collective-permute-start.1) | collective-permute-done | bytes 786464 | tf_op jit(solution)/shard_map/ppermute | solution.py:35
  104.0 0.9 shard_map.90
Async XLA Ops:
  52.9 3.8 %copy-start.4 = (s32[16,4]{0,1:T(4,128)S(1)}, s32[16,4]{0,1:T(4,128)}, u32[]{:S(2)}) copy-start(s32[16,4]{0,1:T(4,128)} %param.15) | copy-start | bytes 772
  52.9 3.9 %copy-start.3 = (s32[16]{0:T(128)S(1)}, s32[16]{0:T(128)}, u32[]{:S(2)}) copy-start(s32[16]{0:T(128)} %size_ref.1) | copy-start | bytes 196
  52.9 19.3 %all-to-all-start.1 = ((bf16[16,384,128]{2,1,0:T(8,128)(2,1)}), bf16[16,384,128]{2,1,0:T(8,128)(2,1)S(1)}, u32[]{:S(2)}, u32[]{:S(2)}) async-start(bf16[16,384,128]{2,1,0:T(8,128)(2,1)} %shard_map.83), calls=%async_computation.1 | async-start | bytes 3145728 | tf_op jit(solution)/shard_map/all_to_all | solution.py:248
  57.5 14.7 %copy-start.2 = (s32[24]{0:T(128)S(1)}, s32[24]{0:T(128)}, u32[]{:S(2)}) copy-start(s32[24]{0:T(128)} %charge_ref.5) | copy-start | bytes 292
  57.5 12.5 %collective-permute-start = (bf16[2,128,512]{2,1,0:T(8,128)(2,1)S(1)}, bf16[2,128,512]{2,1,0:T(8,128)(2,1)S(1)}, u32[]{:S(2)}, u32[]{:S(2)}) collective-permute-start(bf16[2,128,512]{2,1,0:T(8,128)(2,1)S(1)} %shard_map.84.own_ref), channel_id=1, source_target_pairs={{1,0},{2,1},{3,2},{4,3},{5,4},{6,5},{7,6},{9,8},{10,9},{11,10},{12... | collective-permute-start | bytes 786440 | tf_op jit(solution)/shard_map/ppermute | solution.py:35
  70.2 0.8 copy-start
  72.3 14.4 %copy-start.1 = (bf16[4,128,512]{2,1,0:T(8,128)(2,1)S(1)}, bf16[4,128,512]{2,1,0:T(8,128)(2,1)}, u32[]{:S(2)}) copy-start(bf16[4,128,512]{2,1,0:T(8,128)(2,1)} %copy-done) | copy-start | bytes 1572868
  73.5 22.8 %collective-permute-start.2 = (bf16[24,128,128]{2,1,0:T(8,128)(2,1)S(1)}, bf16[24,128,128]{2,1,0:T(8,128)(2,1)S(1)}, u32[]{:S(2)}, u32[]{:S(2)}) collective-permute-start(bf16[24,128,128]{2,1,0:T(8,128)(2,1)S(1)} %get-tuple-element.20), channel_id=1, source_target_pairs={{0,1},{1,2},{2,3},{3,4},{4,5},{5,6},{6,7},{8,9},{9,10},{10,11},{11... | collective-permute-start | bytes 2359304 | tf_op jit(solution)/shard_map/ppermute | solution.py:35
  89.9 14.1 %collective-permute-start.1 = (bf16[24,128,128]{2,1,0:T(8,128)(2,1)S(1)}, bf16[24,128,128]{2,1,0:T(8,128)(2,1)S(1)}, u32[]{:S(2)}, u32[]{:S(2)}) collective-permute-start(bf16[24,128,128]{2,1,0:T(8,128)(2,1)S(1)} %get-tuple-element.18), channel_id=1, source_target_pairs={{0,1},{1,2},{2,3},{3,4},{4,5},{5,6},{6,7},{8,9},{9,10},{10,11},{11... | collective-permute-start | bytes 2359304 | tf_op jit(solution)/shard_map/ppermute | solution.py:35

commit v2 on v1

--- a/solution.py
+++ b/solution.py
@@ -13,7 +13,7 @@
 SMEM = pl.BlockSpec(memory_space=pltpu.SMEM)
 HBM = pl.BlockSpec(memory_space=pltpu.MemorySpace.HBM)
 DMA = pltpu.SemaphoreType.DMA
-COEF_AT, SITE_AT, MESSAGE = 128, 160, 224
+SITE_AT, COEF_AT = 128, 192
 
 
 def call(body, out, ins, outs, scratch=(), flops=0, moved=4 << 20, grant=16 << 20, **more):
@@ -50,11 +50,9 @@
         for b in range(8):
             sf_ref[b * 8 + zh * 2 : b * 8 + zh * 2 + 2, :] = piece[2 * b : 2 * b + 2, :]
     site = sf_ref[...].astype(BF16)
-    coef = c_ref[...].astype(F32)
-    coef = jnp.concatenate([coef, jnp.zeros((SITE_AT - COEF_AT - c_ref.shape[0], 128), F32)], axis=0).astype(BF16)
     for d in range(planes):
-        out_ref[d, COEF_AT:SITE_AT, :] = coef
-        out_ref[d, SITE_AT:, :] = site
+        out_ref[d, SITE_AT:COEF_AT, :] = site
+        out_ref[d, COEF_AT:, :] = c_ref[...]
 
 
 def mix_kernel(a_ref, out_hbm, gf_ref, cf_ref, out_ref, sems):
@@ -147,32 +145,40 @@
     early_ref[3] = turned(own_ref, 1, (3,))
 
 
-def front_kernel(charge_ref, r_ref, op_ref, early_ref, out_ref, comb_ref):
+def front_kernel(core, charge_ref, r_ref, op_ref, early_ref, out_ref):
+    @pl.when(lax.axis_index("core") == core)
+    def _():
+        def step(h, _):
+            pair = combine(r_ref, op_ref, h, 1)
+            parts = [inner(pair[e], early_ref[charge_ref[2 * h + e]]) for e in range(2)]
+            two = product(early_ref[3], joined(parts, 0, 128))
+            for e in range(2):
+                out_ref[2 * h + e] = two[:, e * 128 : (e + 1) * 128].astype(BF16)
+            return 0
+
+        lax.fori_loop(0, op_ref.shape[0] // 2, step, 0, unroll=12)
+
+
+def front_far(*refs):
+    front_kernel(1, *refs)
+
+
+def front_near(*refs):
+    front_kernel(0, *refs)
+
+
+def last_kernel(charge_ref, r_ref, zero_ref, one_ref, pool_ref, out_ref, comb_ref, other_ref, left_ref):
+    left_ref[...] = jnp.concatenate([turned(pool_ref, 1, (1, 2)), turned(pool_ref, 0, (3,))], axis=1)
+
     def step(h, _):
-        pair = combine(r_ref, op_ref, h, 1)
-        parts = []
-        for e in range(2):
-            comb_ref[2 * h + e] = pair[e]
-            parts.append(inner(pair[e], early_ref[charge_ref[2 * h + e]]))
-        two = product(early_ref[3], joined(parts, 0, 128))
-        for e in range(2):
-            out_ref[2 * h + e] = two[:, e * 128 : (e + 1) * 128].astype(BF16)
-        return 0
-
-    lax.fori_loop(0, op_ref.shape[0] // 2, step, 0, unroll=12)
-
-
-def last_kernel(charge_ref, r_ref, op_ref, one_ref, pool_ref, out_ref, comb_ref, left_ref):
-    left_ref[...] = jnp.concatenate([turned(pool_ref, 1, (1, 2)), turned(pool_ref, 0, (3,))], axis=1)
-
-    def step(h, _):
-        pair = combine(r_ref, op_ref, h, 0)
+        pair = combine(r_ref, zero_ref, h, 0)
+        high = combine(r_ref, one_ref, h, 1)
         tall = []
         for e in range(2):
             k = 2 * h + e
             q = charge_ref[k]
-            comb_ref[k] = pair[e]
-            ones = inner(one_ref[k], pool_ref[q + 1, :, 128:384])
+            comb_ref[k], other_ref[k] = pair[e], high[e]
+            ones = inner(high[e], pool_ref[q + 1, :, 128:384])
             two = inner(pair[e], pool_ref[q, :, 384:])
             tall.append(jnp.concatenate([ones[:, :128], ones[:, 128:], two], axis=0))
         total = product(left_ref[...], jnp.concatenate(tall, axis=1))
@@ -204,24 +210,27 @@
     lax.fori_loop(0, one_ref.shape[0] // 2, step, 0, unroll=2)
 
 
-def close(sector, kept_ref, came_ref, out_hbm, done_ref, sems):
+def close(sector, kept_ref, came_refs, out_hbm, done_ref, sems):
     size = kept_ref.shape[0] // 3
     moves = []
     for piece in range(3):
         at = slice(piece * size, (piece + 1) * size)
-        done_ref[at] = (kept_ref[at] + came_ref[at].astype(F32)).astype(BF16)
+        total = kept_ref[at]
+        for ref in came_refs:
+            total = total + ref[at].astype(F32)
+        done_ref[at] = total.astype(BF16)
         moves.append(pltpu.make_async_copy(done_ref.at[at], out_hbm.at[at, sector], sems.at[piece]))
         moves[-1].start()
     for move in moves:
         move.wait()
 
 
-def close_one(kept_ref, came_ref, out_hbm, done_ref, sems):
-    close(1, kept_ref, came_ref, out_hbm, done_ref, sems)
+def close_one(kept_ref, far_ref, near_ref, out_hbm, done_ref, sems):
+    close(1, kept_ref, (far_ref, near_ref), out_hbm, done_ref, sems)
 
 
 def close_zero(kept_ref, came_ref, _, out_hbm, done_ref, sems):
-    close(0, kept_ref, came_ref, out_hbm, done_ref, sems)
+    close(0, kept_ref, (came_ref,), out_hbm, done_ref, sems)
 
 
 def body(site_tensor, operators, one_index, weights, comp_charge, one_charge, sector_size, coupling):
@@ -231,7 +240,7 @@
     far = lax.all_gather(column, "zh", axis=0)
     coef = jnp.where(comp_charge[:, None] == one_charge[None, :], weights, jnp.zeros((), BF16))
     message = call(
-        spread_kernel, sds((16, MESSAGE, 128), BF16), [VMEM, VMEM], VMEM, [pltpu.VMEM((64, 128), F32)]
+        spread_kernel, sds((16, COEF_AT + ops, 128), BF16), [VMEM, VMEM], VMEM, [pltpu.VMEM((64, 128), F32)]
     )(coef, far)
     near = lax.all_to_all(message, PLANE, 0, 0, tiled=True)
     rows = ops * 8
@@ -252,20 +261,20 @@
         pool_kernel, [sds((4, 128, 512), BF16), sds((4, 128, 128), BF16)], [VMEM] * 2, [VMEM] * 2
     )(own, upper)
     zero, one = operators[:, 0], operators[:, 1]
-    leave, comb_one = call(front_kernel, [half, half], [SMEM] + [VMEM] * 3, [VMEM] * 2, flops=flops)(
-        comp_charge, landed, one, early
-    )
-    came_one = shift(leave, 1)
-    leave, comb_zero = call(
-        last_kernel, [half, half], [SMEM] + [VMEM] * 4, [VMEM] * 2, [pltpu.VMEM((128, 384), BF16)], flops=3 * flops
-    )(comp_charge, landed, zero, comb_one, pool)
+    leave = call(front_far, half, [SMEM] + [VMEM] * 3, VMEM, flops=flops)(comp_charge, landed, one, early)
+    came_far = lax.ppermute(leave, GROUP, [(1, 2), (3, 4), (5, 6)])
+    leave = call(front_near, half, [SMEM] + [VMEM] * 3, VMEM, flops=flops)(comp_charge, landed, one, early)
+    came_near = lax.ppermute(leave, GROUP, [(0, 1), (2, 3), (4, 5), (6, 7)])
+    leave, comb_zero, comb_one = call(
+        last_kernel, [half] * 3, [SMEM] + [VMEM] * 4, [VMEM] * 3, [pltpu.VMEM((128, 384), BF16)], flops=3 * flops
+    )(comp_charge, landed, zero, one, pool)
     came_zero = shift(leave, 1)
     first, second = call(
         own_kernel, [wide, wide], [SMEM] + [VMEM] * 3, [VMEM] * 2, [pltpu.VMEM((128, 512), BF16)], flops=4 * flops
     )(comp_charge, comb_one, comb_zero, pool)
     whole = sds((ops, 2, 128, 128), BF16)
     scratch = [pltpu.VMEM((ops, 128, 128), BF16), DMA((3,))]
-    out = call(close_one, whole, [VMEM] * 2, HBM, scratch)(second, came_one)
+    out = call(close_one, whole, [VMEM] * 3, HBM, scratch)(second, came_far, came_near)
     return call(close_zero, whole, [VMEM, VMEM, HBM], HBM, scratch, input_output_aliases={2: 0})(first, came_zero, out)
 
 

time: 105 us -> 104 us (level)
  waiting for transfers between devices: 11 us -> 8.5 us
    ppermute x0 -> x2, starting transfers between devices: none -> 13.6 us  [the longest x1 12.3 us: body(): came_far = lax.ppermute(leave, GROUP, [(1, 2), (3, 4), (5, 6)])]
    ppermute x3 -> x2, starting transfers between devices: 23.1 us -> 10.4 us  [shift(): lax.ppermute(value, GROUP, [(a, a + steps) for a in range(first, last)])]
    ppermute x3 -> x2, waiting for transfers between devices: 9.66 us -> 7.03 us  [shift(): lax.ppermute(value, GROUP, [(a, a + steps) for a in range(first, last)])]
    pallas_call x4 -> x5, Pallas kernels: 5.56 us -> 6.17 us  [the longest x1 3.25 us: body(): call(last_kernel, [half] * 3, [SMEM] + [VMEM] * 4, [VMEM] * 3, [pltpu.VME...]
  transfers between devices with their start and end apart: 4 -> 5, of which waited for: 3 -> 3; matrix products, arithmetic and copies ran while one was open for 1% -> 2% of each run, Pallas kernels for 9% -> 10%
where the time goes in v2:
time: 104 us
  blocking collectives  48.9 us (47%)
  starting transfers between devices  27.7 us (27%)
  Pallas kernels  14.4 us (14%)
  waiting for transfers between devices  8.5 us (8%)
  local copies, waits for them, and re-layouts  2.38 us (2%)
  other arithmetic  1.71 us (2%)
    all_gather x1, blocking collectives, body(): far = lax.all_gather(column, 'zh', axis=0)  31.7 us
    all_to_all x1, blocking collectives, body(): near = lax.all_to_all(message, PLANE, 0, 0, tiled=True)  17.2 us
    ppermute x1, starting transfers between devices, body(): came_far = lax.ppermute(leave, GROUP, [(1, 2), (3, 4), (5, 6)])  12.3 us
    ppermute x2, starting transfers between devices, shift(): lax.ppermute(value, GROUP, [(a, a + steps) for a in range(first, last)])  10.4 us
    ppermute x2, waiting for transfers between devices, shift(): lax.ppermute(value, GROUP, [(a, a + steps) for a in range(first, last)])  7.03 us
    pallas_call x1, Pallas kernels, body(): call(own_kernel, [wide, wide], [SMEM] + [VMEM] * 3, [VMEM] * 2, [pltpu.VM...  4.5 us
    all_to_all x1, starting transfers between devices, body(): landed = lax.all_to_all(mixed, PLANE, 0, 0, tiled=True)  3.72 us
    pallas_call x1, Pallas kernels, body(): call(last_kernel, [half] * 3, [SMEM] + [VMEM] * 4, [VMEM] * 3, [pltpu.VME...  3.25 us
  transfers between devices with their start and end apart: 5, of which 3 were waited for; matrix products, arithmetic and copies ran while one was open for 2% of the time, Pallas kernels for 10%

profile of v2, /device:TPU:1, one launch (start us, length us, event | category | flops | bytes accessed | tf_op | source)
XLA Modules:
  0.0 103.8 jit_solution(12520485183433558127)
XLA Ops:
  0.0 0.9 pad_maximum_fusion
  0.9 31.7 %all-gather = bf16[2112,128]{1,0:T(8,128)(2,1)S(1)} all-gather(bf16[528,128]{1,0:T(8,128)(2,1)S(1)} %pad_maximum_fusion), channel_id=2, replica_groups=mesh['x'=4,'y'=4,'zh'=4,'zl'=4,'core'=2] {'zh'}, dimensions={0}, use_global_device_ids=true | all-gather | bytes 675840 | tf_op jit(solution)/shard_map/all_gather | solution.py:240
  32.6 0.8 compare_select_fusion.c_ref
  33.4 0.1 shard_map.82
  33.5 17.2 %all_to_all.10.a_ref = bf16[16,216,128]{2,1,0:T(8,128)(2,1)S(1)} all-to-all(bf16[16,216,128]{2,1,0:T(8,128)(2,1)S(1)} %shard_map.82), channel_id=1, replica_groups=mesh['x'=4,'y'=4,'zh'=4,'zl'=4,'core'=2] {'x','y'}, dimensions={0} | all-to-all | bytes 1769472 | tf_op jit(solution)/shard_map/all_to_all | solution.py:245
  50.8 2.0 %shard_map.83 = bf16[16,384,128]{2,1,0:T(8,128)(2,1)} custom-call(bf16[16,216,128]{2,1,0:T(8,128)(2,1)S(1)} %all_to_all.10.a_ref), custom_call_target="tpu_custom_call" | custom-call | bytes 4194304 | tf_op jit(solution)/shard_map/pallas_call | solution.py:250
  52.7 0.0 copy-start.4
  52.7 0.0 copy-start.3
  52.7 3.7 %all-to-all-start.1 = ((bf16[16,384,128]{2,1,0:T(8,128)(2,1)}), bf16[16,384,128]{2,1,0:T(8,128)(2,1)S(1)}, u32[]{:S(2)}, u32[]{:S(2)}) async-start(bf16[16,384,128]{2,1,0:T(8,128)(2,1)} %shard_map.83), calls=%async_computation.1 | async-start | bytes 3145728 | tf_op jit(solution)/shard_map/all_to_all | solution.py:257
  56.5 0.0 copy-done.4
  56.5 0.1 copy.12.coupling_ref
  56.6 0.0 copy-done.3
  56.6 0.8 shard_map.84.own_ref
  57.3 0.0 copy-start.2
  57.3 8.0 %collective-permute-start = (bf16[2,128,512]{2,1,0:T(8,128)(2,1)S(1)}, bf16[2,128,512]{2,1,0:T(8,128)(2,1)S(1)}, u32[]{:S(2)}, u32[]{:S(2)}) collective-permute-start(bf16[2,128,512]{2,1,0:T(8,128)(2,1)S(1)} %shard_map.84.own_ref), channel_id=1, source_target_pairs={{1,0},{2,1},{3,2},{4,3},{5,4},{6,5},{7,6},{9,8},{10,9},{11,10},{12... | collective-permute-start | bytes 786440 | tf_op jit(solution)/shard_map/ppermute | solution.py:35
  65.4 1.5 %slice_bitcast_fusion = (bf16[24,128,128]{2,1,0:T(8,128)(2,1)S(1)}, bf16[24,128,128]{2,1,0:T(8,128)(2,1)S(1)}) fusion(bf16[24,2,128,128]{3,2,1,0:T(8,128)(2,1)} %param.9), kind=kLoop, calls=%fused_computation | loop fusion | bytes 3145728 | tf_op jit(solution)/shard_map/squeeze | solution.py:263
  66.8 2.8 %collective-permute-done.up_ref = bf16[2,128,512]{2,1,0:T(8,128)(2,1)S(1)} collective-permute-done((bf16[2,128,512]{2,1,0:T(8,128)(2,1)S(1)}, bf16[2,128,512]{2,1,0:T(8,128)(2,1)S(1)}, u32[]{:S(2)}, u32[]{:S(2)}) %collective-permute-start) | collective-permute-done | bytes 262176 | tf_op jit(solution)/shard_map/ppermute | solution.py:35
  69.6 0.1 shard_map.85
  69.8 0.0 copy-start
  69.8 0.8 copy-done
  70.6 1.5 %all-to-all-done.1.r_ref.refs_1_ = bf16[16,384,128]{2,1,0:T(8,128)(2,1)S(1)} async-done(((bf16[16,384,128]{2,1,0:T(8,128)(2,1)}), bf16[16,384,128]{2,1,0:T(8,128)(2,1)S(1)}, u32[]{:S(2)}, u32[]{:S(2)}) %all-to-all-start.1) | async-done | bytes 1572896 | tf_op jit(solution)/shard_map/all_to_all | solution.py:257
  72.0 0.0 copy-done.2
  72.0 1.2 %shard_map.88 = bf16[24,128,128]{2,1,0:T(8,128)(2,1)S(1)} custom-call(s32[24]{0:T(128)S(1)} %copy-done.2, bf16[16,384,128]{2,1,0:T(8,128)(2,1)S(1)} %all-to-all-done.1.r_ref.refs_1_, bf16[24,128,128]{2,1,0:T(8,128)(2,1)S(1)} %get-tuple-element.19.one_ref.refs_2_, bf16[4,128,128]{2,1,0:T(8,128)(2,1)S(1)} %get-tuple-element.18.refs_3_), custom_call_target="tpu_custom_call" | custom-call | flops 201326592 | bytes 4194304 | tf_op jit(solution)/shard_map/pallas_call | solution.py:264
  73.3 0.0 copy-start.1
  73.3 12.3 %collective-permute-start.2 = (bf16[24,128,128]{2,1,0:T(8,128)(2,1)S(1)}, bf16[24,128,128]{2,1,0:T(8,128)(2,1)S(1)}, u32[]{:S(2)}, u32[]{:S(2)}) collective-permute-start(bf16[24,128,128]{2,1,0:T(8,128)(2,1)S(1)} %shard_map.88), channel_id=1, source_target_pairs={{1,2},{3,4},{5,6},{9,10},{11,12},{13,14},{17,18},{19,20},{21,22},{... | collective-permute-start | bytes 2359304 | tf_op jit(solution)/shard_map/ppermute | solution.py:265
  85.6 0.6 shard_map.89
  86.1 1.3 %collective-permute-start.3 = (bf16[24,128,128]{2,1,0:T(8,128)(2,1)S(1)}, bf16[24,128,128]{2,1,0:T(8,128)(2,1)S(1)}, u32[]{:S(2)}, u32[]{:S(2)}) collective-permute-start(bf16[24,128,128]{2,1,0:T(8,128)(2,1)S(1)} %shard_map.89), channel_id=1, source_target_pairs={{0,1},{2,3},{4,5},{6,7},{8,9},{10,11},{12,13},{14,15},{16,17},{18,... | collective-permute-start | bytes 2359304 | tf_op jit(solution)/shard_map/ppermute | solution.py:267
  87.4 0.0 copy-done.1
  87.5 3.2 %shard_map.86 = (bf16[24,128,128]{2,1,0:T(8,128)(2,1)S(1)}, bf16[24,128,128]{2,1,0:T(8,128)(2,1)S(1)}, bf16[24,128,128]{2,1,0:T(8,128)(2,1)S(1)}) custom-call(s32[24]{0:T(128)S(1)} %copy-done.2, bf16[16,384,128]{2,1,0:T(8,128)(2,1)S(1)} %all-to-all-done.1.r_ref.refs_1_, bf16[24,128,128]{2,1,0:T(8,128)(2,1)S(1)} %get-tuple-element.20.zero_ref, ...), custom_call_target="tpu_custom_call" | custom-call | flops 603979776 | bytes 4194304 | tf_op jit(solution)/shard_map/pallas_call | solution.py:268
  90.7 2.4 %collective-permute-start.1 = (bf16[24,128,128]{2,1,0:T(8,128)(2,1)S(1)}, bf16[24,128,128]{2,1,0:T(8,128)(2,1)S(1)}, u32[]{:S(2)}, u32[]{:S(2)}) collective-permute-start(bf16[24,128,128]{2,1,0:T(8,128)(2,1)S(1)} %get-tuple-element.16), channel_id=1, source_target_pairs={{0,1},{1,2},{2,3},{3,4},{4,5},{5,6},{6,7},{8,9},{9,10},{10,11},{11... | collective-permute-start | bytes 2359304 | tf_op jit(solution)/shard_map/ppermute | solution.py:35
  93.1 4.5 %shard_map.87 = (f32[24,128,128]{2,1,0:T(8,128)S(1)}, f32[24,128,128]{2,1,0:T(8,128)S(1)}) custom-call(s32[24]{0:T(128)S(1)} %copy-done.2, bf16[24,128,128]{2,1,0:T(8,128)(2,1)S(1)} %get-tuple-element.13.one_ref, bf16[24,128,128]{2,1,0:T(8,128)(2,1)S(1)} %get-tuple-element.14.zero_ref, bf16[4,128,512]{2,1,0:T(8,128)(2,1)S(1)} %copy-done.1), custom_call_target="tpu_custom_call" | custom-call | flops 805306368 | bytes 4194304 | tf_op jit(solution)/shard_map/pallas_call | solution.py:272
  97.6 0.0 collective-permute-done.2.far_ref
  97.6 0.0 collective-permute-done.3.near_ref
  97.6 1.0 shard_map.90._
  98.6 4.2 %collective-permute-done.1.came_ref = bf16[24,128,128]{2,1,0:T(8,128)(2,1)S(1)} collective-permute-done((bf16[24,128,128]{2,1,0:T(8,128)(2,1)S(1)}, bf16[24,128,128]{2,1,0:T(8,128)(2,1)S(1)}, u32[]{:S(2)}, u32[]{:S(2)}) %collective-permute-start.1) | collective-permute-done | bytes 786464 | tf_op jit(solution)/shard_map/ppermute | solution.py:35
  102.9 0.9 shard_map.91
Async XLA Ops:
  52.7 3.8 %copy-start.4 = (s32[16,4]{0,1:T(4,128)S(1)}, s32[16,4]{0,1:T(4,128)}, u32[]{:S(2)}) copy-start(s32[16,4]{0,1:T(4,128)} %param.15) | copy-start | bytes 772
  52.7 3.8 %copy-start.3 = (s32[16]{0:T(128)S(1)}, s32[16]{0:T(128)}, u32[]{:S(2)}) copy-start(s32[16]{0:T(128)} %size_ref.1) | copy-start | bytes 196
  52.7 19.3 %all-to-all-start.1 = ((bf16[16,384,128]{2,1,0:T(8,128)(2,1)}), bf16[16,384,128]{2,1,0:T(8,128)(2,1)S(1)}, u32[]{:S(2)}, u32[]{:S(2)}) async-start(bf16[16,384,128]{2,1,0:T(8,128)(2,1)} %shard_map.83), calls=%async_computation.1 | async-start | bytes 3145728 | tf_op jit(solution)/shard_map/all_to_all | solution.py:257
  57.3 14.7 %copy-start.2 = (s32[24]{0:T(128)S(1)}, s32[24]{0:T(128)}, u32[]{:S(2)}) copy-start(s32[24]{0:T(128)} %refs_0_.3) | copy-start | bytes 292
  57.3 12.3 %collective-permute-start = (bf16[2,128,512]{2,1,0:T(8,128)(2,1)S(1)}, bf16[2,128,512]{2,1,0:T(8,128)(2,1)S(1)}, u32[]{:S(2)}, u32[]{:S(2)}) collective-permute-start(bf16[2,128,512]{2,1,0:T(8,128)(2,1)S(1)} %shard_map.84.own_ref), channel_id=1, source_target_pairs={{1,0},{2,1},{3,2},{4,3},{5,4},{6,5},{7,6},{9,8},{10,9},{11,10},{12... | collective-permute-start | bytes 786440 | tf_op jit(solution)/shard_map/ppermute | solution.py:35
  69.8 0.8 copy-start
  73.3 14.2 %copy-start.1 = (bf16[4,128,512]{2,1,0:T(8,128)(2,1)S(1)}, bf16[4,128,512]{2,1,0:T(8,128)(2,1)}, u32[]{:S(2)}) copy-start(bf16[4,128,512]{2,1,0:T(8,128)(2,1)} %copy-done) | copy-start | bytes 1572868
  73.3 24.3 %collective-permute-start.2 = (bf16[24,128,128]{2,1,0:T(8,128)(2,1)S(1)}, bf16[24,128,128]{2,1,0:T(8,128)(2,1)S(1)}, u32[]{:S(2)}, u32[]{:S(2)}) collective-permute-start(bf16[24,128,128]{2,1,0:T(8,128)(2,1)S(1)} %shard_map.88), channel_id=1, source_target_pairs={{1,2},{3,4},{5,6},{9,10},{11,12},{13,14},{17,18},{19,20},{21,22},{... | collective-permute-start | bytes 2359304 | tf_op jit(solution)/shard_map/ppermute | solution.py:265
  86.1 11.5 %collective-permute-start.3 = (bf16[24,128,128]{2,1,0:T(8,128)(2,1)S(1)}, bf16[24,128,128]{2,1,0:T(8,128)(2,1)S(1)}, u32[]{:S(2)}, u32[]{:S(2)}) collective-permute-start(bf16[24,128,128]{2,1,0:T(8,128)(2,1)S(1)} %shard_map.89), channel_id=1, source_target_pairs={{0,1},{2,3},{4,5},{6,7},{8,9},{10,11},{12,13},{14,15},{16,17},{18,... | collective-permute-start | bytes 2359304 | tf_op jit(solution)/shard_map/ppermute | solution.py:267
  90.7 12.2 %collective-permute-start.1 = (bf16[24,128,128]{2,1,0:T(8,128)(2,1)S(1)}, bf16[24,128,128]{2,1,0:T(8,128)(2,1)S(1)}, u32[]{:S(2)}, u32[]{:S(2)}) collective-permute-start(bf16[24,128,128]{2,1,0:T(8,128)(2,1)S(1)} %get-tuple-element.16), channel_id=1, source_target_pairs={{0,1},{1,2},{2,3},{3,4},{4,5},{5,6},{6,7},{8,9},{9,10},{10,11},{11... | collective-permute-start | bytes 2359304 | tf_op jit(solution)/shard_map/ppermute | solution.py:35

commit v3 on v1

--- a/solution.py
+++ b/solution.py
@@ -13,7 +13,7 @@
 SMEM = pl.BlockSpec(memory_space=pltpu.SMEM)
 HBM = pl.BlockSpec(memory_space=pltpu.MemorySpace.HBM)
 DMA = pltpu.SemaphoreType.DMA
-COEF_AT, SITE_AT, MESSAGE = 128, 160, 224
+SITE_AT, COEF_AT = 128, 192
 
 
 def call(body, out, ins, outs, scratch=(), flops=0, moved=4 << 20, grant=16 << 20, **more):
@@ -50,11 +50,9 @@
         for b in range(8):
             sf_ref[b * 8 + zh * 2 : b * 8 + zh * 2 + 2, :] = piece[2 * b : 2 * b + 2, :]
     site = sf_ref[...].astype(BF16)
-    coef = c_ref[...].astype(F32)
-    coef = jnp.concatenate([coef, jnp.zeros((SITE_AT - COEF_AT - c_ref.shape[0], 128), F32)], axis=0).astype(BF16)
     for d in range(planes):
-        out_ref[d, COEF_AT:SITE_AT, :] = coef
-        out_ref[d, SITE_AT:, :] = site
+        out_ref[d, SITE_AT:COEF_AT, :] = site
+        out_ref[d, COEF_AT:, :] = c_ref[...]
 
 
 def mix_kernel(a_ref, out_hbm, gf_ref, cf_ref, out_ref, sems):
@@ -147,13 +145,10 @@
     early_ref[3] = turned(own_ref, 1, (3,))
 
 
-def front_kernel(charge_ref, r_ref, op_ref, early_ref, out_ref, comb_ref):
+def front(charge_ref, r_ref, op_ref, early_ref, out_ref):
     def step(h, _):
         pair = combine(r_ref, op_ref, h, 1)
-        parts = []
-        for e in range(2):
-            comb_ref[2 * h + e] = pair[e]
-            parts.append(inner(pair[e], early_ref[charge_ref[2 * h + e]]))
+        parts = [inner(pair[e], early_ref[charge_ref[2 * h + e]]) for e in range(2)]
         two = product(early_ref[3], joined(parts, 0, 128))
         for e in range(2):
             out_ref[2 * h + e] = two[:, e * 128 : (e + 1) * 128].astype(BF16)
@@ -162,17 +157,44 @@
     lax.fori_loop(0, op_ref.shape[0] // 2, step, 0, unroll=12)
 
 
-def last_kernel(charge_ref, r_ref, op_ref, one_ref, pool_ref, out_ref, comb_ref, left_ref):
+def front_far(*refs):
+    @pl.when(lax.axis_index("core") == 1)
+    def _():
+        front(*refs)
+
+
+def front_near(charge_ref, r_ref, op_ref, early_ref, came_ref, out_ref):
+    @pl.when(lax.axis_index("core") == 0)
+    def _():
+        front(charge_ref, r_ref, op_ref, early_ref, out_ref)
+
+    @pl.when(lax.axis_index("core") == 1)
+    def _():
+        out_ref[...] = came_ref[...]
+
+
+def pick_kernel(leave_ref, came_ref, out_ref):
+    @pl.when(lax.axis_index("core") == 0)
+    def _():
+        out_ref[...] = leave_ref[...]
+
+    @pl.when(lax.axis_index("core") == 1)
+    def _():
+        out_ref[...] = came_ref[...]
+
+
+def last_kernel(charge_ref, r_ref, zero_ref, one_ref, pool_ref, out_ref, comb_ref, other_ref, left_ref):
     left_ref[...] = jnp.concatenate([turned(pool_ref, 1, (1, 2)), turned(pool_ref, 0, (3,))], axis=1)
 
     def step(h, _):
-        pair = combine(r_ref, op_ref, h, 0)
+        pair = combine(r_ref, zero_ref, h, 0)
+        high = combine(r_ref, one_ref, h, 1)
         tall = []
         for e in range(2):
             k = 2 * h + e
             q = charge_ref[k]
-            comb_ref[k] = pair[e]
-            ones = inner(one_ref[k], pool_ref[q + 1, :, 128:384])
+            comb_ref[k], other_ref[k] = pair[e], high[e]
+            ones = inner(high[e], pool_ref[q + 1, :, 128:384])
             two = inner(pair[e], pool_ref[q, :, 384:])
             tall.append(jnp.concatenate([ones[:, :128], ones[:, 128:], two], axis=0))
         total = product(left_ref[...], jnp.concatenate(tall, axis=1))
@@ -231,7 +253,7 @@
     far = lax.all_gather(column, "zh", axis=0)
     coef = jnp.where(comp_charge[:, None] == one_charge[None, :], weights, jnp.zeros((), BF16))
     message = call(
-        spread_kernel, sds((16, MESSAGE, 128), BF16), [VMEM, VMEM], VMEM, [pltpu.VMEM((64, 128), F32)]
+        spread_kernel, sds((16, COEF_AT + ops, 128), BF16), [VMEM, VMEM], VMEM, [pltpu.VMEM((64, 128), F32)]
     )(coef, far)
     near = lax.all_to_all(message, PLANE, 0, 0, tiled=True)
     rows = ops * 8
@@ -252,17 +274,22 @@
         pool_kernel, [sds((4, 128, 512), BF16), sds((4, 128, 128), BF16)], [VMEM] * 2, [VMEM] * 2
     )(own, upper)
     zero, one = operators[:, 0], operators[:, 1]
-    leave, comb_one = call(front_kernel, [half, half], [SMEM] + [VMEM] * 3, [VMEM] * 2, flops=flops)(
-        comp_charge, landed, one, early
-    )
-    came_one = shift(leave, 1)
-    leave, comb_zero = call(
-        last_kernel, [half, half], [SMEM] + [VMEM] * 4, [VMEM] * 2, [pltpu.VMEM((128, 384), BF16)], flops=3 * flops
-    )(comp_charge, landed, zero, comb_one, pool)
-    came_zero = shift(leave, 1)
+    onward = [(1, 3), (3, 5), (5, 7)]
+    swap = [(i, i ^ 1) for i in range(8)]
+    ins = [SMEM] + [VMEM] * 3
+    leave = call(front_far, half, ins, VMEM, flops=flops)(comp_charge, landed, one, early)
+    came = lax.ppermute(leave, GROUP, onward)
+    leave, comb_zero, comb_one = call(
+        last_kernel, [half] * 3, [SMEM] + [VMEM] * 4, [VMEM] * 3, [pltpu.VMEM((128, 384), BF16)], flops=3 * flops
+    )(comp_charge, landed, zero, one, pool)
+    came_far = lax.ppermute(leave, GROUP, onward)
+    near_one = call(front_near, half, ins + [VMEM], VMEM, flops=flops)(comp_charge, landed, one, early, came)
+    came_one = lax.ppermute(near_one, GROUP, swap)
     first, second = call(
-        own_kernel, [wide, wide], [SMEM] + [VMEM] * 3, [VMEM] * 2, [pltpu.VMEM((128, 512), BF16)], flops=4 * flops
+        own_kernel, [wide, wide], ins, [VMEM] * 2, [pltpu.VMEM((128, 512), BF16)], flops=4 * flops
     )(comp_charge, comb_one, comb_zero, pool)
+    near_zero = call(pick_kernel, half, [VMEM] * 2, VMEM)(leave, came_far)
+    came_zero = lax.ppermute(near_zero, GROUP, swap)
     whole = sds((ops, 2, 128, 128), BF16)
     scratch = [pltpu.VMEM((ops, 128, 128), BF16), DMA((3,))]
     out = call(close_one, whole, [VMEM] * 2, HBM, scratch)(second, came_one)

time: 105 us -> 107 us (1.019)
  waiting for transfers between devices: 11 us -> 13.8 us
  starting transfers between devices: 26.8 us -> 25.2 us
    ppermute x3 -> x1, starting transfers between devices: 23.1 us -> 8.01 us  [shift(): lax.ppermute(value, GROUP, [(a, a + steps) for a in range(first, last)])]
    ppermute x0 -> x4, starting transfers between devices: none -> 13.5 us  [the longest x1 7.76 us: body(): came = lax.ppermute(leave, GROUP, onward)]
    ppermute x0 -> x4, waiting for transfers between devices: none -> 9.57 us  [the longest x1 5.89 us: body(): came_far = lax.ppermute(leave, GROUP, onward)]
    ppermute x3 -> x1, waiting for transfers between devices: 9.66 us -> 2.79 us  [shift(): lax.ppermute(value, GROUP, [(a, a + steps) for a in range(first, last)])]
    pallas_call x4 -> x6, Pallas kernels: 9.12 us -> 9.78 us  [the longest x1 4.5 us: body(): call(own_kernel, [wide, wide], ins, [VMEM] * 2, [pltpu.VMEM((128, 512), B...]
  transfers between devices with their start and end apart: 4 -> 6, of which waited for: 3 -> 4; matrix products, arithmetic and copies ran while one was open for 1% -> 1% of each run, Pallas kernels for 9% -> 10%
where the time goes in v3:
time: 107 us
  blocking collectives  48.9 us (46%)
  starting transfers between devices  25.2 us (24%)
  Pallas kernels  14.5 us (14%)
  waiting for transfers between devices  13.8 us (13%)
  local copies, waits for them, and re-layouts  2.38 us (2%)
  other arithmetic  1.71 us (2%)
    all_gather x1, blocking collectives, body(): far = lax.all_gather(column, 'zh', axis=0)  31.7 us
    all_to_all x1, blocking collectives, body(): near = lax.all_to_all(message, PLANE, 0, 0, tiled=True)  17.2 us
    ppermute x1, starting transfers between devices, shift(): lax.ppermute(value, GROUP, [(a, a + steps) for a in range(first, last)])  8.01 us
    ppermute x1, starting transfers between devices, body(): came = lax.ppermute(leave, GROUP, onward)  7.76 us
    ppermute x1, waiting for transfers between devices, body(): came_far = lax.ppermute(leave, GROUP, onward)  5.89 us
    pallas_call x1, Pallas kernels, body(): call(own_kernel, [wide, wide], ins, [VMEM] * 2, [pltpu.VMEM((128, 512), B...  4.5 us
    all_to_all x1, starting transfers between devices, body(): landed = lax.all_to_all(mixed, PLANE, 0, 0, tiled=True)  3.72 us
    ppermute x1, waiting for transfers between devices, body(): came = lax.ppermute(leave, GROUP, onward)  3.68 us
  transfers between devices with their start and end apart: 6, of which 4 were waited for; matrix products, arithmetic and copies ran while one was open for 1% of the time, Pallas kernels for 10%

profile of v3, /device:TPU:1, one launch (start us, length us, event | category | flops | bytes accessed | tf_op | source)
XLA Modules:
  0.0 106.8 jit_solution(16673672036591331327)
XLA Ops:
  0.0 0.9 pad_maximum_fusion
  0.9 31.7 %all-gather = bf16[2112,128]{1,0:T(8,128)(2,1)S(1)} all-gather(bf16[528,128]{1,0:T(8,128)(2,1)S(1)} %pad_maximum_fusion), channel_id=2, replica_groups=mesh['x'=4,'y'=4,'zh'=4,'zl'=4,'core'=2] {'zh'}, dimensions={0}, use_global_device_ids=true | all-gather | bytes 675840 | tf_op jit(solution)/shard_map/all_gather | solution.py:253
  32.6 0.8 compare_select_fusion.c_ref
  33.4 0.1 shard_map.82
  33.5 17.2 %all_to_all.10.a_ref = bf16[16,216,128]{2,1,0:T(8,128)(2,1)S(1)} all-to-all(bf16[16,216,128]{2,1,0:T(8,128)(2,1)S(1)} %shard_map.82), channel_id=1, replica_groups=mesh['x'=4,'y'=4,'zh'=4,'zl'=4,'core'=2] {'x','y'}, dimensions={0} | all-to-all | bytes 1769472 | tf_op jit(solution)/shard_map/all_to_all | solution.py:258
  50.8 2.0 %shard_map.83 = bf16[16,384,128]{2,1,0:T(8,128)(2,1)} custom-call(bf16[16,216,128]{2,1,0:T(8,128)(2,1)S(1)} %all_to_all.10.a_ref), custom_call_target="tpu_custom_call" | custom-call | bytes 4194304 | tf_op jit(solution)/shard_map/pallas_call | solution.py:263
  52.7 0.0 copy-start.4
  52.7 0.0 copy-start.3
  52.7 3.7 %all-to-all-start.1 = ((bf16[16,384,128]{2,1,0:T(8,128)(2,1)}), bf16[16,384,128]{2,1,0:T(8,128)(2,1)S(1)}, u32[]{:S(2)}, u32[]{:S(2)}) async-start(bf16[16,384,128]{2,1,0:T(8,128)(2,1)} %shard_map.83), calls=%async_computation.1 | async-start | bytes 3145728 | tf_op jit(solution)/shard_map/all_to_all | solution.py:270
  56.5 0.0 copy-done.4
  56.5 0.1 copy.12.coupling_ref
  56.6 0.0 copy-done.3
  56.6 0.8 shard_map.84.own_ref
  57.3 0.0 copy-start.2
  57.3 8.0 %collective-permute-start = (bf16[2,128,512]{2,1,0:T(8,128)(2,1)S(1)}, bf16[2,128,512]{2,1,0:T(8,128)(2,1)S(1)}, u32[]{:S(2)}, u32[]{:S(2)}) collective-permute-start(bf16[2,128,512]{2,1,0:T(8,128)(2,1)S(1)} %shard_map.84.own_ref), channel_id=1, source_target_pairs={{1,0},{2,1},{3,2},{4,3},{5,4},{6,5},{7,6},{9,8},{10,9},{11,10},{12... | collective-permute-start | bytes 786440 | tf_op jit(solution)/shard_map/ppermute | solution.py:35
  65.4 1.5 %slice_bitcast_fusion = (bf16[24,128,128]{2,1,0:T(8,128)(2,1)S(1)}, bf16[24,128,128]{2,1,0:T(8,128)(2,1)S(1)}) fusion(bf16[24,2,128,128]{3,2,1,0:T(8,128)(2,1)} %param.9), kind=kLoop, calls=%fused_computation | loop fusion | bytes 3145728 | tf_op jit(solution)/shard_map/squeeze | solution.py:276
  66.8 2.8 %collective-permute-done.up_ref = bf16[2,128,512]{2,1,0:T(8,128)(2,1)S(1)} collective-permute-done((bf16[2,128,512]{2,1,0:T(8,128)(2,1)S(1)}, bf16[2,128,512]{2,1,0:T(8,128)(2,1)S(1)}, u32[]{:S(2)}, u32[]{:S(2)}) %collective-permute-start) | collective-permute-done | bytes 262176 | tf_op jit(solution)/shard_map/ppermute | solution.py:35
  69.6 0.1 shard_map.85
  69.8 0.0 copy-start
  69.8 0.8 copy-done
  70.6 1.5 %all-to-all-done.1.r_ref.refs_1_ = bf16[16,384,128]{2,1,0:T(8,128)(2,1)S(1)} async-done(((bf16[16,384,128]{2,1,0:T(8,128)(2,1)}), bf16[16,384,128]{2,1,0:T(8,128)(2,1)S(1)}, u32[]{:S(2)}, u32[]{:S(2)}) %all-to-all-start.1) | async-done | bytes 1572896 | tf_op jit(solution)/shard_map/all_to_all | solution.py:270
  72.0 0.0 copy-done.2
  72.0 0.0 copy-start.1
  72.0 1.2 %shard_map.89 = bf16[24,128,128]{2,1,0:T(8,128)(2,1)S(1)} custom-call(s32[24]{0:T(128)S(1)} %copy-done.2, bf16[16,384,128]{2,1,0:T(8,128)(2,1)S(1)} %all-to-all-done.1.r_ref.refs_1_, bf16[24,128,128]{2,1,0:T(8,128)(2,1)S(1)} %get-tuple-element.19.one_ref.refs_2_.op_ref, bf16[4,128,128]{2,1,0:T(8,128)(2,1)S(1)} %get-tuple-element.18.refs_3_.early_ref), custom_call_target="tpu_custom_call" | custom-call | flops 201326592 | bytes 4194304 | tf_op jit(solution)/shard_map/pallas_call | solution.py:280
  73.3 7.8 %collective-permute-start.3 = (bf16[24,128,128]{2,1,0:T(8,128)(2,1)S(1)}, bf16[24,128,128]{2,1,0:T(8,128)(2,1)S(1)}, u32[]{:S(2)}, u32[]{:S(2)}) collective-permute-start(bf16[24,128,128]{2,1,0:T(8,128)(2,1)S(1)} %shard_map.89), channel_id=1, source_target_pairs={{1,3},{3,5},{5,7},{9,11},{11,13},{13,15},{17,19},{19,21},{21,23},{... | collective-permute-start | bytes 2359304 | tf_op jit(solution)/shard_map/ppermute | solution.py:281
  81.0 0.0 copy-done.1
  81.1 3.2 %shard_map.86 = (bf16[24,128,128]{2,1,0:T(8,128)(2,1)S(1)}, bf16[24,128,128]{2,1,0:T(8,128)(2,1)S(1)}, bf16[24,128,128]{2,1,0:T(8,128)(2,1)S(1)}) custom-call(s32[24]{0:T(128)S(1)} %copy-done.2, bf16[16,384,128]{2,1,0:T(8,128)(2,1)S(1)} %all-to-all-done.1.r_ref.refs_1_, bf16[24,128,128]{2,1,0:T(8,128)(2,1)S(1)} %get-tuple-element.20.zero_ref, ...), custom_call_target="tpu_custom_call" | custom-call | flops 603979776 | bytes 4194304 | tf_op jit(solution)/shard_map/pallas_call | solution.py:282
  84.3 1.9 %collective-permute-start.1 = (bf16[24,128,128]{2,1,0:T(8,128)(2,1)S(1)}, bf16[24,128,128]{2,1,0:T(8,128)(2,1)S(1)}, u32[]{:S(2)}, u32[]{:S(2)}) collective-permute-start(bf16[24,128,128]{2,1,0:T(8,128)(2,1)S(1)} %get-tuple-element.16.leave_ref), channel_id=1, source_target_pairs={{1,3},{3,5},{5,7},{9,11},{11,13},{13,15},{17,19},{19,21},{21,23},{... | collective-permute-start | bytes 2359304 | tf_op jit(solution)/shard_map/ppermute | solution.py:285
  86.2 3.7 %collective-permute-done.3.came_ref = bf16[24,128,128]{2,1,0:T(8,128)(2,1)S(1)} collective-permute-done((bf16[24,128,128]{2,1,0:T(8,128)(2,1)S(1)}, bf16[24,128,128]{2,1,0:T(8,128)(2,1)S(1)}, u32[]{:S(2)}, u32[]{:S(2)}) %collective-permute-start.3) | collective-permute-done | bytes 786464 | tf_op jit(solution)/shard_map/ppermute | solution.py:281
  89.9 0.6 shard_map.90
  90.5 1.9 %collective-permute-start.4 = (bf16[24,128,128]{2,1,0:T(8,128)(2,1)S(1)}, bf16[24,128,128]{2,1,0:T(8,128)(2,1)S(1)}, u32[]{:S(2)}, u32[]{:S(2)}) collective-permute-start(bf16[24,128,128]{2,1,0:T(8,128)(2,1)S(1)} %shard_map.90), channel_id=1, source_target_pairs={{0,1},{1,0},{2,3},{3,2},{4,5},{5,4},{6,7},{7,6},{8,9},{9,8},{10,11... | collective-permute-start | bytes 2359304 | tf_op jit(solution)/shard_map/ppermute | solution.py:287
  92.5 5.9 %collective-permute-done.1.came_ref = bf16[24,128,128]{2,1,0:T(8,128)(2,1)S(1)} collective-permute-done((bf16[24,128,128]{2,1,0:T(8,128)(2,1)S(1)}, bf16[24,128,128]{2,1,0:T(8,128)(2,1)S(1)}, u32[]{:S(2)}, u32[]{:S(2)}) %collective-permute-start.1) | collective-permute-done | bytes 786464 | tf_op jit(solution)/shard_map/ppermute | solution.py:285
  98.3 0.1 shard_map.88
  98.4 1.9 %collective-permute-start.2 = (bf16[24,128,128]{2,1,0:T(8,128)(2,1)S(1)}, bf16[24,128,128]{2,1,0:T(8,128)(2,1)S(1)}, u32[]{:S(2)}, u32[]{:S(2)}) collective-permute-start(bf16[24,128,128]{2,1,0:T(8,128)(2,1)S(1)} %shard_map.88), channel_id=1, source_target_pairs={{0,1},{1,0},{2,3},{3,2},{4,5},{5,4},{6,7},{7,6},{8,9},{9,8},{10,11... | collective-permute-start | bytes 2359304 | tf_op jit(solution)/shard_map/ppermute | solution.py:292
  100.3 4.5 %shard_map.87 = (f32[24,128,128]{2,1,0:T(8,128)S(1)}, f32[24,128,128]{2,1,0:T(8,128)S(1)}) custom-call(s32[24]{0:T(128)S(1)} %copy-done.2, bf16[24,128,128]{2,1,0:T(8,128)(2,1)S(1)} %get-tuple-element.13.one_ref, bf16[24,128,128]{2,1,0:T(8,128)(2,1)S(1)} %get-tuple-element.14.zero_ref, bf16[4,128,512]{2,1,0:T(8,128)(2,1)S(1)} %copy-done.1), custom_call_target="tpu_custom_call" | custom-call | flops 805306368 | bytes 4194304 | tf_op jit(solution)/shard_map/pallas_call | solution.py:288
  104.8 0.0 collective-permute-done.4.came_ref
  104.8 0.9 shard_map.91._
  105.8 0.0 collective-permute-done.2.came_ref
  105.8 0.9 shard_map.92
Async XLA Ops:
  52.7 3.8 %copy-start.4 = (s32[16,4]{0,1:T(4,128)S(1)}, s32[16,4]{0,1:T(4,128)}, u32[]{:S(2)}) copy-start(s32[16,4]{0,1:T(4,128)} %param.15) | copy-start | bytes 772
  52.7 3.8 %copy-start.3 = (s32[16]{0:T(128)S(1)}, s32[16]{0:T(128)}, u32[]{:S(2)}) copy-start(s32[16]{0:T(128)} %size_ref.1) | copy-start | bytes 196
  52.7 19.3 %all-to-all-start.1 = ((bf16[16,384,128]{2,1,0:T(8,128)(2,1)}), bf16[16,384,128]{2,1,0:T(8,128)(2,1)S(1)}, u32[]{:S(2)}, u32[]{:S(2)}) async-start(bf16[16,384,128]{2,1,0:T(8,128)(2,1)} %shard_map.83), calls=%async_computation.1 | async-start | bytes 3145728 | tf_op jit(solution)/shard_map/all_to_all | solution.py:270
  57.3 14.7 %copy-start.2 = (s32[24]{0:T(128)S(1)}, s32[24]{0:T(128)}, u32[]{:S(2)}) copy-start(s32[24]{0:T(128)} %charge_ref.5) | copy-start | bytes 292
  57.3 12.3 %collective-permute-start = (bf16[2,128,512]{2,1,0:T(8,128)(2,1)S(1)}, bf16[2,128,512]{2,1,0:T(8,128)(2,1)S(1)}, u32[]{:S(2)}, u32[]{:S(2)}) collective-permute-start(bf16[2,128,512]{2,1,0:T(8,128)(2,1)S(1)} %shard_map.84.own_ref), channel_id=1, source_target_pairs={{1,0},{2,1},{3,2},{4,3},{5,4},{6,5},{7,6},{9,8},{10,9},{11,10},{12... | collective-permute-start | bytes 786440 | tf_op jit(solution)/shard_map/ppermute | solution.py:35
  69.8 0.8 copy-start
  72.0 9.0 %copy-start.1 = (bf16[4,128,512]{2,1,0:T(8,128)(2,1)S(1)}, bf16[4,128,512]{2,1,0:T(8,128)(2,1)}, u32[]{:S(2)}) copy-start(bf16[4,128,512]{2,1,0:T(8,128)(2,1)} %copy-done) | copy-start | bytes 1572868
  73.3 16.6 %collective-permute-start.3 = (bf16[24,128,128]{2,1,0:T(8,128)(2,1)S(1)}, bf16[24,128,128]{2,1,0:T(8,128)(2,1)S(1)}, u32[]{:S(2)}, u32[]{:S(2)}) collective-permute-start(bf16[24,128,128]{2,1,0:T(8,128)(2,1)S(1)} %shard_map.89), channel_id=1, source_target_pairs={{1,3},{3,5},{5,7},{9,11},{11,13},{13,15},{17,19},{19,21},{21,23},{... | collective-permute-start | bytes 2359304 | tf_op jit(solution)/shard_map/ppermute | solution.py:281
  84.3 14.0 %collective-permute-start.1 = (bf16[24,128,128]{2,1,0:T(8,128)(2,1)S(1)}, bf16[24,128,128]{2,1,0:T(8,128)(2,1)S(1)}, u32[]{:S(2)}, u32[]{:S(2)}) collective-permute-start(bf16[24,128,128]{2,1,0:T(8,128)(2,1)S(1)} %get-tuple-element.16.leave_ref), channel_id=1, source_target_pairs={{1,3},{3,5},{5,7},{9,11},{11,13},{13,15},{17,19},{19,21},{21,23},{... | collective-permute-start | bytes 2359304 | tf_op jit(solution)/shard_map/ppermute | solution.py:285
  90.5 14.3 %collective-permute-start.4 = (bf16[24,128,128]{2,1,0:T(8,128)(2,1)S(1)}, bf16[24,128,128]{2,1,0:T(8,128)(2,1)S(1)}, u32[]{:S(2)}, u32[]{:S(2)}) collective-permute-start(bf16[24,128,128]{2,1,0:T(8,128)(2,1)S(1)} %shard_map.90), channel_id=1, source_target_pairs={{0,1},{1,0},{2,3},{3,2},{4,5},{5,4},{6,7},{7,6},{8,9},{9,8},{10,11... | collective-permute-start | bytes 2359304 | tf_op jit(solution)/shard_map/ppermute | solution.py:287
  98.4 7.4 %collective-permute-start.2 = (bf16[24,128,128]{2,1,0:T(8,128)(2,1)S(1)}, bf16[24,128,128]{2,1,0:T(8,128)(2,1)S(1)}, u32[]{:S(2)}, u32[]{:S(2)}) collective-permute-start(bf16[24,128,128]{2,1,0:T(8,128)(2,1)S(1)} %shard_map.88), channel_id=1, source_target_pairs={{0,1},{1,0},{2,3},{3,2},{4,5},{5,4},{6,7},{7,6},{8,9},{9,8},{10,11... | collective-permute-start | bytes 2359304 | tf_op jit(solution)/shard_map/ppermute | solution.py:292

commit v4 on v3

--- a/solution.py
+++ b/solution.py
@@ -173,16 +173,6 @@
         out_ref[...] = came_ref[...]
 
 
-def pick_kernel(leave_ref, came_ref, out_ref):
-    @pl.when(lax.axis_index("core") == 0)
-    def _():
-        out_ref[...] = leave_ref[...]
-
-    @pl.when(lax.axis_index("core") == 1)
-    def _():
-        out_ref[...] = came_ref[...]
-
-
 def last_kernel(charge_ref, r_ref, zero_ref, one_ref, pool_ref, out_ref, comb_ref, other_ref, left_ref):
     left_ref[...] = jnp.concatenate([turned(pool_ref, 1, (1, 2)), turned(pool_ref, 0, (3,))], axis=1)
 
@@ -223,7 +213,7 @@
             second_ref[k] = second[:, at]
         return 0
 
-    lax.fori_loop(0, one_ref.shape[0] // 2, step, 0, unroll=2)
+    lax.fori_loop(0, one_ref.shape[0] // 2, step, 0, unroll=6)
 
 
 def close(sector, kept_ref, came_ref, out_hbm, done_ref, sems):
@@ -282,14 +272,12 @@
     leave, comb_zero, comb_one = call(
         last_kernel, [half] * 3, [SMEM] + [VMEM] * 4, [VMEM] * 3, [pltpu.VMEM((128, 384), BF16)], flops=3 * flops
     )(comp_charge, landed, zero, one, pool)
-    came_far = lax.ppermute(leave, GROUP, onward)
+    came_zero = shift(leave, 1)
     near_one = call(front_near, half, ins + [VMEM], VMEM, flops=flops)(comp_charge, landed, one, early, came)
     came_one = lax.ppermute(near_one, GROUP, swap)
     first, second = call(
         own_kernel, [wide, wide], ins, [VMEM] * 2, [pltpu.VMEM((128, 512), BF16)], flops=4 * flops
     )(comp_charge, comb_one, comb_zero, pool)
-    near_zero = call(pick_kernel, half, [VMEM] * 2, VMEM)(leave, came_far)
-    came_zero = lax.ppermute(near_zero, GROUP, swap)
     whole = sds((ops, 2, 128, 128), BF16)
     scratch = [pltpu.VMEM((ops, 128, 128), BF16), DMA((3,))]
     out = call(close_one, whole, [VMEM] * 2, HBM, scratch)(second, came_one)

time: 107 us -> 110 us (1.028)
  waiting for transfers between devices: 13.8 us -> 17.1 us
    ppermute x2 -> x0, waiting for transfers between devices: 5.89 us -> none  [the longest x1 5.89 us: body(): came_far = lax.ppermute(leave, GROUP, onward)]
    ppermute x1, waiting for transfers between devices: 3.68 us -> 8.87 us  [body(): came = lax.ppermute(leave, GROUP, onward)]
    ppermute x1 -> x2, starting transfers between devices: 8.01 us -> 12.2 us  [shift(): lax.ppermute(value, GROUP, [(a, a + steps) for a in range(first, last)])]
    ppermute x1 -> x2, waiting for transfers between devices: 2.79 us -> 6.79 us  [shift(): lax.ppermute(value, GROUP, [(a, a + steps) for a in range(first, last)])]
    ppermute x2 -> x0, starting transfers between devices: 3.84 us -> none  [the longest x1 1.92 us: body(): came_far = lax.ppermute(leave, GROUP, onward)]
  transfers between devices with their start and end apart: 6 -> 5, of which waited for: 4 -> 4; matrix products, arithmetic and copies ran while one was open for 1% -> 1% of each run, Pallas kernels for 10% -> 8%
where the time goes in v4:
time: 110 us
  blocking collectives  48.9 us (44%)
  starting transfers between devices  25.7 us (23%)
  waiting for transfers between devices  17.1 us (16%)
  Pallas kernels  13.9 us (13%)
  local copies, waits for them, and re-layouts  2.38 us (2%)
  other arithmetic  1.71 us (2%)
    all_gather x1, blocking collectives, body(): far = lax.all_gather(column, 'zh', axis=0)  31.7 us
    all_to_all x1, blocking collectives, body(): near = lax.all_to_all(message, PLANE, 0, 0, tiled=True)  17.2 us
    ppermute x2, starting transfers between devices, shift(): lax.ppermute(value, GROUP, [(a, a + steps) for a in range(first, last)])  12.2 us
    ppermute x1, waiting for transfers between devices, body(): came = lax.ppermute(leave, GROUP, onward)  8.87 us
    ppermute x1, starting transfers between devices, body(): came = lax.ppermute(leave, GROUP, onward)  7.89 us
    ppermute x2, waiting for transfers between devices, shift(): lax.ppermute(value, GROUP, [(a, a + steps) for a in range(first, last)])  6.79 us
    pallas_call x1, Pallas kernels, body(): call(own_kernel, [wide, wide], ins, [VMEM] * 2, [pltpu.VMEM((128, 512), B...  3.94 us
    all_to_all x1, starting transfers between devices, body(): landed = lax.all_to_all(mixed, PLANE, 0, 0, tiled=True)  3.72 us
  transfers between devices with their start and end apart: 5, of which 4 were waited for; matrix products, arithmetic and copies ran while one was open for 1% of the time, Pallas kernels for 8%

profile of v4, /device:TPU:1, one launch (start us, length us, event | category | flops | bytes accessed | tf_op | source)
XLA Modules:
  0.0 109.9 jit_solution(10107871566396131220)
XLA Ops:
  0.0 0.9 pad_maximum_fusion
  0.9 31.7 %all-gather = bf16[2112,128]{1,0:T(8,128)(2,1)S(1)} all-gather(bf16[528,128]{1,0:T(8,128)(2,1)S(1)} %pad_maximum_fusion), channel_id=2, replica_groups=mesh['x'=4,'y'=4,'zh'=4,'zl'=4,'core'=2] {'zh'}, dimensions={0}, use_global_device_ids=true | all-gather | bytes 675840 | tf_op jit(solution)/shard_map/all_gather | solution.py:243
  32.6 0.8 compare_select_fusion.c_ref
  33.4 0.1 shard_map.82
  33.5 17.2 %all_to_all.10.a_ref = bf16[16,216,128]{2,1,0:T(8,128)(2,1)S(1)} all-to-all(bf16[16,216,128]{2,1,0:T(8,128)(2,1)S(1)} %shard_map.82), channel_id=1, replica_groups=mesh['x'=4,'y'=4,'zh'=4,'zl'=4,'core'=2] {'x','y'}, dimensions={0} | all-to-all | bytes 1769472 | tf_op jit(solution)/shard_map/all_to_all | solution.py:248
  50.8 2.0 %shard_map.83 = bf16[16,384,128]{2,1,0:T(8,128)(2,1)} custom-call(bf16[16,216,128]{2,1,0:T(8,128)(2,1)S(1)} %all_to_all.10.a_ref), custom_call_target="tpu_custom_call" | custom-call | bytes 4194304 | tf_op jit(solution)/shard_map/pallas_call | solution.py:253
  52.7 0.0 copy-start.4
  52.7 0.0 copy-start.3
  52.7 3.7 %all-to-all-start.1 = ((bf16[16,384,128]{2,1,0:T(8,128)(2,1)}), bf16[16,384,128]{2,1,0:T(8,128)(2,1)S(1)}, u32[]{:S(2)}, u32[]{:S(2)}) async-start(bf16[16,384,128]{2,1,0:T(8,128)(2,1)} %shard_map.83), calls=%async_computation.1 | async-start | bytes 3145728 | tf_op jit(solution)/shard_map/all_to_all | solution.py:260
  56.5 0.0 copy-done.4
  56.5 0.1 copy.12.coupling_ref
  56.6 0.0 copy-done.3
  56.6 0.8 shard_map.84.own_ref
  57.3 0.0 copy-start.2
  57.3 8.0 %collective-permute-start = (bf16[2,128,512]{2,1,0:T(8,128)(2,1)S(1)}, bf16[2,128,512]{2,1,0:T(8,128)(2,1)S(1)}, u32[]{:S(2)}, u32[]{:S(2)}) collective-permute-start(bf16[2,128,512]{2,1,0:T(8,128)(2,1)S(1)} %shard_map.84.own_ref), channel_id=1, source_target_pairs={{1,0},{2,1},{3,2},{4,3},{5,4},{6,5},{7,6},{9,8},{10,9},{11,10},{12... | collective-permute-start | bytes 786440 | tf_op jit(solution)/shard_map/ppermute | solution.py:35
  65.4 1.5 %slice_bitcast_fusion = (bf16[24,128,128]{2,1,0:T(8,128)(2,1)S(1)}, bf16[24,128,128]{2,1,0:T(8,128)(2,1)S(1)}) fusion(bf16[24,2,128,128]{3,2,1,0:T(8,128)(2,1)} %param.9), kind=kLoop, calls=%fused_computation | loop fusion | bytes 3145728 | tf_op jit(solution)/shard_map/squeeze | solution.py:266
  66.8 2.8 %collective-permute-done.up_ref = bf16[2,128,512]{2,1,0:T(8,128)(2,1)S(1)} collective-permute-done((bf16[2,128,512]{2,1,0:T(8,128)(2,1)S(1)}, bf16[2,128,512]{2,1,0:T(8,128)(2,1)S(1)}, u32[]{:S(2)}, u32[]{:S(2)}) %collective-permute-start) | collective-permute-done | bytes 262176 | tf_op jit(solution)/shard_map/ppermute | solution.py:35
  69.6 0.1 shard_map.85
  69.8 0.0 copy-start
  69.8 0.8 copy-done
  70.6 1.5 %all-to-all-done.1.r_ref.refs_1_ = bf16[16,384,128]{2,1,0:T(8,128)(2,1)S(1)} async-done(((bf16[16,384,128]{2,1,0:T(8,128)(2,1)}), bf16[16,384,128]{2,1,0:T(8,128)(2,1)S(1)}, u32[]{:S(2)}, u32[]{:S(2)}) %all-to-all-start.1) | async-done | bytes 1572896 | tf_op jit(solution)/shard_map/all_to_all | solution.py:260
  72.0 0.0 copy-done.2
  72.0 1.2 %shard_map.88 = bf16[24,128,128]{2,1,0:T(8,128)(2,1)S(1)} custom-call(s32[24]{0:T(128)S(1)} %copy-done.2, bf16[16,384,128]{2,1,0:T(8,128)(2,1)S(1)} %all-to-all-done.1.r_ref.refs_1_, bf16[24,128,128]{2,1,0:T(8,128)(2,1)S(1)} %get-tuple-element.19.one_ref.refs_2_.op_ref, bf16[4,128,128]{2,1,0:T(8,128)(2,1)S(1)} %get-tuple-element.18.refs_3_.early_ref), custom_call_target="tpu_custom_call" | custom-call | flops 201326592 | bytes 4194304 | tf_op jit(solution)/shard_map/pallas_call | solution.py:270
  73.3 0.0 copy-start.1
  73.3 7.9 %collective-permute-start.2 = (bf16[24,128,128]{2,1,0:T(8,128)(2,1)S(1)}, bf16[24,128,128]{2,1,0:T(8,128)(2,1)S(1)}, u32[]{:S(2)}, u32[]{:S(2)}) collective-permute-start(bf16[24,128,128]{2,1,0:T(8,128)(2,1)S(1)} %shard_map.88), channel_id=1, source_target_pairs={{1,3},{3,5},{5,7},{9,11},{11,13},{13,15},{17,19},{19,21},{21,23},{... | collective-permute-start | bytes 2359304 | tf_op jit(solution)/shard_map/ppermute | solution.py:271
  81.2 8.9 %collective-permute-done.2.came_ref = bf16[24,128,128]{2,1,0:T(8,128)(2,1)S(1)} collective-permute-done((bf16[24,128,128]{2,1,0:T(8,128)(2,1)S(1)}, bf16[24,128,128]{2,1,0:T(8,128)(2,1)S(1)}, u32[]{:S(2)}, u32[]{:S(2)}) %collective-permute-start.2) | collective-permute-done | bytes 786464 | tf_op jit(solution)/shard_map/ppermute | solution.py:271
  90.1 0.6 shard_map.89
  90.7 1.9 %collective-permute-start.3 = (bf16[24,128,128]{2,1,0:T(8,128)(2,1)S(1)}, bf16[24,128,128]{2,1,0:T(8,128)(2,1)S(1)}, u32[]{:S(2)}, u32[]{:S(2)}) collective-permute-start(bf16[24,128,128]{2,1,0:T(8,128)(2,1)S(1)} %shard_map.89), channel_id=1, source_target_pairs={{0,1},{1,0},{2,3},{3,2},{4,5},{5,4},{6,7},{7,6},{8,9},{9,8},{10,11... | collective-permute-start | bytes 2359304 | tf_op jit(solution)/shard_map/ppermute | solution.py:277
  92.6 0.0 copy-done.1
  92.6 3.2 %shard_map.86 = (bf16[24,128,128]{2,1,0:T(8,128)(2,1)S(1)}, bf16[24,128,128]{2,1,0:T(8,128)(2,1)S(1)}, bf16[24,128,128]{2,1,0:T(8,128)(2,1)S(1)}) custom-call(s32[24]{0:T(128)S(1)} %copy-done.2, bf16[16,384,128]{2,1,0:T(8,128)(2,1)S(1)} %all-to-all-done.1.r_ref.refs_1_, bf16[24,128,128]{2,1,0:T(8,128)(2,1)S(1)} %get-tuple-element.20.zero_ref, ...), custom_call_target="tpu_custom_call" | custom-call | flops 603979776 | bytes 4194304 | tf_op jit(solution)/shard_map/pallas_call | solution.py:272
  95.9 4.2 %collective-permute-start.1 = (bf16[24,128,128]{2,1,0:T(8,128)(2,1)S(1)}, bf16[24,128,128]{2,1,0:T(8,128)(2,1)S(1)}, u32[]{:S(2)}, u32[]{:S(2)}) collective-permute-start(bf16[24,128,128]{2,1,0:T(8,128)(2,1)S(1)} %get-tuple-element.16), channel_id=1, source_target_pairs={{0,1},{1,2},{2,3},{3,4},{4,5},{5,6},{6,7},{8,9},{9,10},{10,11},{11... | collective-permute-start | bytes 2359304 | tf_op jit(solution)/shard_map/ppermute | solution.py:35
  100.1 3.9 %shard_map.87 = (f32[24,128,128]{2,1,0:T(8,128)S(1)}, f32[24,128,128]{2,1,0:T(8,128)S(1)}) custom-call(s32[24]{0:T(128)S(1)} %copy-done.2, bf16[24,128,128]{2,1,0:T(8,128)(2,1)S(1)} %get-tuple-element.13.one_ref, bf16[24,128,128]{2,1,0:T(8,128)(2,1)S(1)} %get-tuple-element.14.zero_ref, bf16[4,128,512]{2,1,0:T(8,128)(2,1)S(1)} %copy-done.1), custom_call_target="tpu_custom_call" | custom-call | flops 805306368 | bytes 4194304 | tf_op jit(solution)/shard_map/pallas_call | solution.py:278
  104.0 0.0 collective-permute-done.3.came_ref
  104.0 0.9 shard_map.90._
  105.0 4.0 %collective-permute-done.1.came_ref = bf16[24,128,128]{2,1,0:T(8,128)(2,1)S(1)} collective-permute-done((bf16[24,128,128]{2,1,0:T(8,128)(2,1)S(1)}, bf16[24,128,128]{2,1,0:T(8,128)(2,1)S(1)}, u32[]{:S(2)}, u32[]{:S(2)}) %collective-permute-start.1) | collective-permute-done | bytes 786464 | tf_op jit(solution)/shard_map/ppermute | solution.py:35
  109.0 0.9 shard_map.91
Async XLA Ops:
  52.7 3.8 %copy-start.4 = (s32[16,4]{0,1:T(4,128)S(1)}, s32[16,4]{0,1:T(4,128)}, u32[]{:S(2)}) copy-start(s32[16,4]{0,1:T(4,128)} %param.15) | copy-start | bytes 772
  52.7 3.8 %copy-start.3 = (s32[16]{0:T(128)S(1)}, s32[16]{0:T(128)}, u32[]{:S(2)}) copy-start(s32[16]{0:T(128)} %size_ref.1) | copy-start | bytes 196
  52.7 19.3 %all-to-all-start.1 = ((bf16[16,384,128]{2,1,0:T(8,128)(2,1)}), bf16[16,384,128]{2,1,0:T(8,128)(2,1)S(1)}, u32[]{:S(2)}, u32[]{:S(2)}) async-start(bf16[16,384,128]{2,1,0:T(8,128)(2,1)} %shard_map.83), calls=%async_computation.1 | async-start | bytes 3145728 | tf_op jit(solution)/shard_map/all_to_all | solution.py:260
  57.3 14.7 %copy-start.2 = (s32[24]{0:T(128)S(1)}, s32[24]{0:T(128)}, u32[]{:S(2)}) copy-start(s32[24]{0:T(128)} %charge_ref.5) | copy-start | bytes 292
  57.3 12.3 %collective-permute-start = (bf16[2,128,512]{2,1,0:T(8,128)(2,1)S(1)}, bf16[2,128,512]{2,1,0:T(8,128)(2,1)S(1)}, u32[]{:S(2)}, u32[]{:S(2)}) collective-permute-start(bf16[2,128,512]{2,1,0:T(8,128)(2,1)S(1)} %shard_map.84.own_ref), channel_id=1, source_target_pairs={{1,0},{2,1},{3,2},{4,3},{5,4},{6,5},{7,6},{9,8},{10,9},{11,10},{12... | collective-permute-start | bytes 786440 | tf_op jit(solution)/shard_map/ppermute | solution.py:35
  69.8 0.8 copy-start
  73.3 19.3 %copy-start.1 = (bf16[4,128,512]{2,1,0:T(8,128)(2,1)S(1)}, bf16[4,128,512]{2,1,0:T(8,128)(2,1)}, u32[]{:S(2)}) copy-start(bf16[4,128,512]{2,1,0:T(8,128)(2,1)} %copy-done) | copy-start | bytes 1572868
  73.3 16.8 %collective-permute-start.2 = (bf16[24,128,128]{2,1,0:T(8,128)(2,1)S(1)}, bf16[24,128,128]{2,1,0:T(8,128)(2,1)S(1)}, u32[]{:S(2)}, u32[]{:S(2)}) collective-permute-start(bf16[24,128,128]{2,1,0:T(8,128)(2,1)S(1)} %shard_map.88), channel_id=1, source_target_pairs={{1,3},{3,5},{5,7},{9,11},{11,13},{13,15},{17,19},{19,21},{21,23},{... | collective-permute-start | bytes 2359304 | tf_op jit(solution)/shard_map/ppermute | solution.py:271
  90.7 13.3 %collective-permute-start.3 = (bf16[24,128,128]{2,1,0:T(8,128)(2,1)S(1)}, bf16[24,128,128]{2,1,0:T(8,128)(2,1)S(1)}, u32[]{:S(2)}, u32[]{:S(2)}) collective-permute-start(bf16[24,128,128]{2,1,0:T(8,128)(2,1)S(1)} %shard_map.89), channel_id=1, source_target_pairs={{0,1},{1,0},{2,3},{3,2},{4,5},{5,4},{6,7},{7,6},{8,9},{9,8},{10,11... | collective-permute-start | bytes 2359304 | tf_op jit(solution)/shard_map/ppermute | solution.py:277
  95.9 13.1 %collective-permute-start.1 = (bf16[24,128,128]{2,1,0:T(8,128)(2,1)S(1)}, bf16[24,128,128]{2,1,0:T(8,128)(2,1)S(1)}, u32[]{:S(2)}, u32[]{:S(2)}) collective-permute-start(bf16[24,128,128]{2,1,0:T(8,128)(2,1)S(1)} %get-tuple-element.16), channel_id=1, source_target_pairs={{0,1},{1,2},{2,3},{3,4},{4,5},{5,6},{6,7},{8,9},{9,10},{10,11},{11... | collective-permute-start | bytes 2359304 | tf_op jit(solution)/shard_map/ppermute | solution.py:35
